TPU v7x, 256 devices: a whole 4x4x8 slice. The times are simulated.
256 devices in a mesh: ctx: 8 (over y_lo, x), tp: 32 (over y_hi, z, core).
Axes of the slice: x: 4, y: 4 (y_hi: 2, y_lo: 2; y = y_hi * 2 + y_lo), z: 8, core: 2. Of those that a mesh axis runs over, the one named last changes fastest.
Arguments:
- normed_rows: bfloat16 [6144, 4096], P(('ctx', 'tp')), may hold values from -6 to 6
- out_grad: bfloat16 [6144, 4096], P(('ctx', 'tp')), may hold values from -6 to 6
- inner_weight: bfloat16 [2, 4096, 8192], P(None, None, 'tp'), may hold values from -0.09375 to 0.09375
- state_weight: bfloat16 [4096, 256], replicated, may hold values from -0.09375 to 0.09375
- step_weight: bfloat16 [4096, 64], P(None, 'tp'), may hold values from -0.09375 to 0.09375
- conv_inner: float32 [4, 8192], P(None, 'tp'), may hold values from -3 to 3
- conv_state: float32 [4, 256], replicated, may hold values from -3 to 3
- step_bias: float32 [64], P('tp'), may hold values from -4 to -1
- decay_log: float32 [64], P('tp')
- norm_gain: float32 [8192], P('tp'), may hold values from 0.1 to 1.9
- out_weight: bfloat16 [8192, 4096], P('tp'), may hold values from -0.0625 to 0.0625
Outputs:
- input_grad: bfloat16 [6144, 4096], P(('ctx', 'tp'))
All inputs are finite; a program needn't handle non-finite values.
Results may differ from a plain program's by a relative error of at most 0.0095.
Values may be sent and summed in bfloat16 or wider, within the bound.
A program may use at most 128 MiB of HBM per device.

v0:
```python
from functools import partial

import jax
import jax.numpy as jnp
from jax import lax
from jax.sharding import PartitionSpec as P

HEAD_DIM = 128
STATE = 128
CONV = 4


EPSILON = 1e-05
EXACT = lax.Precision.HIGHEST


def shifted(value, axis, by):
    length = lax.axis_size(axis)
    pairs = [(i, i + by) for i in range(length) if 0 <= i + by < length]
    return lax.ppermute(value, axis, pairs)


def prefix(value, axis, combine, identity, reverse):
    length, mine = (lax.axis_size(axis), lax.axis_index(axis))
    everything = jax.tree.map(lambda part: lax.all_gather(part, axis), value)
    start = jax.tree.map(
        lambda part, zero: jnp.broadcast_to(jnp.asarray(zero, part.dtype), part.shape),
        value,
        identity,
    )

    def turn(k, before):
        at = length - 1 - k if reverse else k
        reached = at > mine if reverse else at < mine
        new = combine(before, jax.tree.map(lambda part: part[at], everything))
        return jax.tree.map(lambda a, b: jnp.where(reached, a, b), new, before)

    return lax.fori_loop(0, length, turn, start)


def decay_table(log_decay):
    running = jnp.cumsum(log_decay, axis=0)
    length = log_decay.shape[0]
    causal = (
        lax.broadcasted_iota(jnp.int32, (length, length), 0)
        >= lax.broadcasted_iota(jnp.int32, (length, length), 1)
    ).astype(jnp.float32)
    spread_log = running.T[:, :, None] - running.T[:, None, :]
    return (running, jnp.exp(jnp.minimum(spread_log, 0.0)) * causal)


def within_shard(inner_act, step_size, log_decay, b_rows, c_rows, entering):
    running, decays = decay_table(log_decay)
    scores = jnp.dot(c_rows, b_rows.T, precision=EXACT)
    weights = decays * scores[None] * step_size.T[:, None, :]
    local_part = jnp.einsum("hts,shp->thp", weights, inner_act, precision=EXACT)
    carried = (
        jnp.einsum("tn,hpn->thp", c_rows, entering, precision=EXACT) * jnp.exp(running)[:, :, None]
    )
    return local_part + carried


def leaving_state(inner_act, step_size, log_decay, b_rows, entering):
    running = jnp.cumsum(log_decay, axis=0)
    weights = jnp.exp(running[-1][None, :] - running) * step_size
    own_state = jnp.einsum("th,thp,tn->hpn", weights, inner_act, b_rows, precision=EXACT)
    return jnp.exp(running[-1])[:, None, None] * entering + own_state


def conv_pieces(extended, step_raw, kernel, step_bias, decay_rates, inner_width):
    length = step_raw.shape[0]
    blended = jnp.zeros((length, extended.shape[1]), jnp.float32)
    for offset in range(kernel.shape[0]):
        blended = blended + kernel[offset] * extended[offset : offset + length]
    active = jax.nn.silu(blended)
    state_half = (extended.shape[1] - inner_width) // 2
    inner_act = active[:, :inner_width].reshape(length, -1, HEAD_DIM)
    b_rows = active[:, inner_width : inner_width + state_half]
    c_rows = active[:, inner_width + state_half :]
    step_size = jax.nn.softplus(step_raw + step_bias)
    return (inner_act, b_rows, c_rows, step_size, -step_size * decay_rates)


def forward_combine(earlier, later):
    return (earlier[0] * later[0], later[0][:, None, None] * earlier[1] + later[1])


def backward_combine(earlier, later):
    return (earlier[0] * later[0], later[1] + later[0][:, None, None] * earlier[1])


def body(
    normed_rows,
    out_grad,
    inner_weight,
    state_weight,
    step_weight,
    conv_inner,
    conv_state,
    step_bias,
    decay_log,
    norm_gain,
    out_weight,
):
    inner_width = inner_weight.shape[2]
    state_width = state_weight.shape[1]
    head_count = step_bias.shape[0]
    rows_all, grads_all = (
        lax.all_gather(normed_rows, "tp", axis=0, tiled=True),
        lax.all_gather(out_grad, "tp", axis=0, tiled=True),
    )
    projected = jnp.concatenate(
        [
            jnp.dot(rows_all, inner_weight[0], preferred_element_type=jnp.float32),
            jnp.dot(rows_all, inner_weight[1], preferred_element_type=jnp.float32),
            jnp.dot(rows_all, state_weight, preferred_element_type=jnp.float32),
            jnp.dot(rows_all, step_weight, preferred_element_type=jnp.float32),
        ],
        axis=1,
    )
    length = projected.shape[0]
    gate_raw = projected[:, :inner_width].astype(jnp.bfloat16)
    conv_in = projected[:, inner_width : 2 * inner_width + state_width].astype(jnp.bfloat16)
    step_raw = projected[:, 2 * inner_width + state_width :].astype(jnp.bfloat16)
    tail_rows = shifted(conv_in[length - (CONV - 1) :], "ctx", 1)
    extended = jnp.concatenate([tail_rows, conv_in], axis=0).astype(jnp.float32)
    kernel = jnp.concatenate([conv_inner, conv_state], axis=1)
    decay_rates = jnp.exp(decay_log)
    pieces_fn = partial(
        conv_pieces,
        kernel=kernel,
        step_bias=step_bias,
        decay_rates=decay_rates,
        inner_width=inner_width,
    )
    pieces, pull_pieces = jax.vjp(pieces_fn, extended, step_raw.astype(jnp.float32))
    inner_act, b_rows, c_rows, step_size, log_decay = pieces
    zero_state = jnp.zeros((head_count, HEAD_DIM, STATE), jnp.float32)
    own_state = leaving_state(inner_act, step_size, log_decay, b_rows, zero_state)
    shard_decay = jnp.exp(jnp.sum(log_decay, axis=0))
    identity = (jnp.ones_like(shard_decay), jnp.zeros_like(own_state))
    entering = prefix((shard_decay, own_state), "ctx", forward_combine, identity, False)[1]
    scan_out, pull_scan = jax.vjp(
        within_shard, inner_act, step_size, log_decay, b_rows, c_rows, entering
    )
    scan_flat = scan_out.reshape(length, inner_width)
    gate_float = gate_raw.astype(jnp.float32)
    gate_act = jax.nn.silu(gate_float)
    gated_out = scan_flat * gate_act
    out_local = jnp.dot(grads_all, out_weight.T, preferred_element_type=jnp.float32)
    token_totals = lax.psum(
        (
            jnp.sum(gated_out * gated_out, axis=1),
            jnp.sum(norm_gain * out_local * gated_out, axis=1),
        ),
        "tp",
    )
    total_width = inner_width * lax.axis_size("tp")
    inverse = lax.rsqrt(token_totals[0] / total_width + EPSILON)[:, None]
    d_gated = (
        inverse * norm_gain * out_local
        - gated_out * (inverse * inverse * inverse) * (token_totals[1] / total_width)[:, None]
    )
    gate_sigmoid = jax.nn.sigmoid(gate_float)
    d_gate = d_gated * scan_flat * gate_sigmoid * (1.0 + gate_float * (1.0 - gate_sigmoid))
    d_scan = (d_gated * gate_act).reshape(length, head_count, HEAD_DIM)
    d_inner, d_step, d_decay, d_brows, d_crows, d_entering = pull_scan(d_scan)
    leaving_grad = prefix((shard_decay, d_entering), "ctx", backward_combine, identity, True)[1]
    _, pull_leave = jax.vjp(
        partial(leaving_state, entering=entering), inner_act, step_size, log_decay, b_rows
    )
    leave_grads = pull_leave(leaving_grad)
    d_extended, d_step_raw = pull_pieces(
        (
            d_inner + leave_grads[0],
            d_brows + leave_grads[3],
            d_crows,
            d_step + leave_grads[1],
            d_decay + leave_grads[2],
        )
    )
    incoming = shifted(d_extended[: CONV - 1], "ctx", -1)
    d_conv = jnp.concatenate(
        [d_extended[CONV - 1 : length], d_extended[length:] + incoming], axis=0
    )
    d_gate_half = d_gate.astype(jnp.bfloat16)
    d_inner_half = d_conv[:, :inner_width].astype(jnp.bfloat16)
    d_state = d_conv[:, inner_width:]
    d_step_half = d_step_raw.astype(jnp.bfloat16)
    state_float = state_weight.astype(jnp.float32)
    summed_term = jnp.dot(d_gate_half, inner_weight[0].T, preferred_element_type=jnp.float32)
    summed_term = summed_term + jnp.dot(
        d_inner_half, inner_weight[1].T, preferred_element_type=jnp.float32
    )
    summed_term = summed_term + jnp.dot(
        d_step_half, step_weight.T, preferred_element_type=jnp.float32
    )
    summed_term = summed_term + jnp.dot(
        d_state, state_float.T, precision=EXACT, preferred_element_type=jnp.float32
    )
    result = lax.psum_scatter(summed_term, "tp", scatter_dimension=0, tiled=True)
    return result.astype(jnp.bfloat16)


def solution(mesh):
    placed = (
        P(("ctx", "tp"), None),
        P(("ctx", "tp"), None),
        P(None, None, "tp"),
        P(),
        P(None, "tp"),
        P(None, "tp"),
        P(),
        P("tp"),
        P("tp"),
        P("tp"),
        P("tp", None),
    )
    return jax.shard_map(
        body, mesh=mesh, in_specs=placed, out_specs=P(("ctx", "tp"), None), check_vma=False
    )
```

profile of v0, /device:TPU:1, one launch (start us, length us, event | category | flops | bytes accessed | tf_op | source)
XLA Modules:
  0.0 632.0 jit_solution(5437332475264679702)
XLA Ops:
  10.2 98.7 %all-gather.8.cloned.1.call-done = bf16[768,4096]{1,0:T(8,128)(2,1)} async-done(((bf16[24,4096]{1,0:T(8,128)(2,1)}), bf16[768,4096]{1,0:T(8,128)(2,1)}) %all-gather.8.cloned.1.call-update) | async-done | bytes 6291472 | tf_op jit(solution)/shard_map/all_gather | solution.py:109
  108.9 4.6 negate_multiply_fusion
  114.4 4.8 convolution_convert_fusion
  119.2 1.1 copy-done.7
  120.3 2.0 fusion.59
  122.4 3.1 collective-permute-start
  125.9 2.1 collective-permute-done
  128.5 2.6 fusion.46
  131.2 1.1 copy-done.1
  132.4 1.5 convolution_add_fusion.2
  135.1 1.6 fusion.28
  136.7 16.2 %all-reduce.9 = f32[16]{0:T(128)S(1)} all-reduce(f32[16]{0:T(128)S(1)} %exponential_dynamic-update-slice_fusion), channel_id=2, replica_groups=mesh['ctx'=8,'tp'=32] {'ctx'}, use_global_device_ids=true, to_apply=%add.9 | all-reduce | flops 16 | bytes 128
  153.0 49.8 %all-gather.10.cloned.1.call-done = bf16[768,4096]{1,0:T(8,128)(2,1)} async-done(((bf16[24,4096]{1,0:T(8,128)(2,1)}), bf16[768,4096]{1,0:T(8,128)(2,1)}) %all-gather.10.cloned.1.call-update) | async-done | bytes 6291472 | tf_op jit(solution)/shard_map/all_gather | solution.py:110
  202.8 6.4 %fusion.133 = f32[768,256]{0,1:T(8,128)} fusion(bf16[768,4096]{1,0:T(8,128)(2,1)} %all-gather.10.cloned.1.call-done, bf16[256,4096]{1,0:T(8,128)(2,1)} %param.25), kind=kOutput, calls=%fused_computation.185 | convolution fusion | flops 1610612736 | bytes 9175040 | tf_op jit(solution)/shard_map/dot_general | solution.py:150
  209.1 3.4 fusion.97
  212.6 24.6 %all-gather.12.cloned.1.call-done = f32[16,128,128]{2,1,0:T(8,128)} async-done(((f32[2,128,128]{2,1,0:T(8,128)}), f32[16,128,128]{2,1,0:T(8,128)}) %all-gather.12.cloned.1.call-update) | async-done | bytes 1048592 | tf_op jit(solution)/shard_map/all_gather | solution.py:25
  237.2 8.2 %while.30 = (s32[]{:T(128)}, f32[2,128,128]{2,1,0:T(8,128)S(1)}, s32[]{:T(128)}, f32[8,2]{1,0:T(8,128)S(1)}, f32[8,2,128,128]{3,2,1,0:T(8,128)}, /*index=5*/s32[]{:T(128)}, s32[]{:T(128)}) while((s32[]{:T(128)}, f32[2,128,128]{2,1,0:T(8,128)S(1)}, s32[]{:T(128)}, f32[8,2]{1,0:T(8,128)S(1)}, f32[8,2,128,128]{3,2,1,0:T(8,128)}, ...), condition=%wide.region_4.5_spmd.clone, body=%wide.region_3.4_spmd.clone.sunk | while | flops 131076 | bytes 393353 | solution.py:38
  238.2 1.0 fusion.157
  239.2 1.0 fusion.157
  240.3 1.0 fusion.157
  242.3 1.0 fusion.157
  244.4 1.0 fusion.157
  245.4 1.8 fusion.87
  248.1 8.3 %fusion.56 = f32[768,2,128]{0,2,1:T(8,128)S(1)} fusion(f32[768,2,128]{0,2,1:T(8,128)S(1)} %bitcast.194, f32[2,768]{1,0:T(2,128)S(1)} %get-tuple-element.304, f32[768,768]{1,0:T(8,128)} %fusion.97, f32[768,768]{1,0:T(8,128)} %fusion.28, f32[2,768]{1,0:T(2,128)S(1)} %get-tuple-element.302, f32[768,2,128]{0,2,1:T(8,128)S(1)} %fusion.87, ...), kind=kOutput, calls=%fused_computation.66 | convolution fusion | flops 1818230784 | bytes 7096320 | tf_op jit(solution)/shard_map/jvp(hts,shp->thp)/dot_general | solution.py:56
  256.5 6.0 multiply_reduce_fusion.3
  262.4 71.5 %all-reduce.10 = (f32[768]{0:T(1024)S(1)}, f32[768]{0:T(1024)S(1)}) all-reduce(f32[768]{0:T(1024)S(1)} %get-tuple-element.274, f32[768]{0:T(1024)S(1)} %get-tuple-element.273), channel_id=1, replica_groups=mesh['ctx'=8,'tp'=32] {'tp'}, use_global_device_ids=true, to_apply=%region_8.9 | all-reduce | flops 1536 | bytes 12288 | tf_op jit(solution)/shard_map/psum | solution.py:151
  334.0 2.3 multiply_reduce_fusion.1
  337.2 2.4 fusion.77
  339.7 10.2 %fusion.14 = (f32[768,768]{1,0:T(8,128)}, f32[2,768]{1,0:T(2,128)}, f32[2,768,768]{2,1,0:T(8,128)S(1)}) fusion(f32[2,768]{1,0:T(2,128)S(1)} %get-tuple-element.304, f32[768,768]{1,0:T(8,128)} %fusion.28, f32[2,768]{1,0:T(2,128)S(1)} %get-tuple-element.302, f32[768,768]{1,0:T(8,128)} %fusion.97, f32[2,128,768]{2,1,0:T(8,128)} %bitcast.198, ...), kind=kOutput, calls=%fused_computation.20 | convolution fusion | flops 1831401984 | bytes 13387776 | tf_op jit(solution)/shard_map/transpose(jvp(hts,shp->thp))/dot_general | solution.py:56
  350.4 2.5 reduce-window.24
  353.8 1.8 convolution_bitcast_fusion.1
  355.7 4.4 convolution_add_fusion.1
  360.7 6.4 %fusion.29 = f32[768,4096]{1,0:T(8,128)} fusion(bf16[768,256]{0,1:T(8,128)(2,1)S(1)} %fusion.75, bf16[2,4096,256]{2,1,0:T(8,128)(2,1)S(1)} %copy-done.9), kind=kOutput, calls=%fused_computation.37 | convolution fusion | flops 1610612736 | bytes 15073280 | tf_op jit(solution)/shard_map/dot_general | solution.py:191
  367.1 3.1 all-gather.14.cloned.1.call-done
  370.2 14.0 %while.31 = (s32[]{:T(128)}, f32[2,128,128]{2,1,0:T(8,128)S(1)}, s32[]{:T(128)}, f32[8,2,128,128]{3,2,1,0:T(8,128)}, f32[8,2]{1,0:T(8,128)}, /*index=5*/s32[]{:T(128)}, s32[]{:T(128)}, s32[]{:T(128)}, s32[]{:T(128)}) while((s32[]{:T(128)}, f32[2,128,128]{2,1,0:T(8,128)S(1)}, s32[]{:T(128)}, f32[8,2,128,128]{3,2,1,0:T(8,128)}, ...), condition=%wide.region_11.12_spmd.clone, body=%wide.region_10.11_spmd.clone.sunk | while | flops 131080 | bytes 393415 | solution.py:38
  384.8 2.1 convolution_bitcast_fusion
  386.9 3.1 multiply_reduce_fusion
  390.2 7.6 %fusion.53 = f32[768,2,128]{0,2,1:T(8,128)} fusion(f32[2,128,768]{2,1,0:T(8,128)} %bitcast.200, f32[2,768]{1,0:T(2,128)} %copy-done.42, f32[768,768]{1,0:T(8,128)} %fusion.97, f32[768,768]{1,0:T(8,128)} %fusion.28, f32[2,768]{1,0:T(2,128)S(1)} %get-tuple-element.302, f32[768,2,128]{0,2,1:T(8,128)} %get-tuple-element.322, f32[768,2]{0,1:T(2,128)} %copy-done.22), kind=kOutput, calls=%fused_computation.65 | convolution fusion | flops 1818230784 | bytes 7096320 | tf_op jit(solution)/shard_map/transpose(jvp(hts,shp->thp))/dot_general | solution.py:56
  398.2 2.5 reduce-window.26
  401.0 3.3 convolution_add_fusion
  405.7 1.5 collective-permute-start.1
  407.3 6.5 %fusion.116 = f32[768,4096]{1,0:T(8,128)} fusion(bf16[4096,2]{0,1:T(2,128)(2,1)S(1)} %copy-done.21, f32[768,2]{0,1:T(2,128)S(1)} %get-tuple-element.319, f32[1,2,6,128]{3,2,1,0:T(8,128)S(1)} %add_bitcast_fusion, f32[768,2]{0,1:T(2,128)S(1)} %get-tuple-element.321, f32[2,768]{1,0:T(2,128)S(1)} %copy-done.41, f32[2]{0:T(128)S(1)} %copy-done.40, ...), kind=kOutput, calls=%fused_computation.166 | convolution fusion | flops 12612096 | bytes 12630032 | tf_op jit(solution)/shard_map/dot_general | solution.py:195
  413.8 1.5 pad_add_fusion
  416.9 1.6 copy-done.10
  418.6 6.4 %fusion.33 = f32[768,4096]{1,0:T(8,128)} fusion(bf16[2,4096,256]{2,1,0:T(8,128)(2,1)S(1)} %copy-done.10, f32[765,512]{0,1:T(8,128)S(1)} %slice.123, f32[3,512]{0,1:T(8,128)S(1)} %add_add_fusion.1), kind=kOutput, calls=%fused_computation.41 | convolution fusion | flops 1611399168 | bytes 16515072 | tf_op jit(solution)/shard_map/dot_general | solution.py:192
  424.9 23.0 %add_add_fusion = f32[768,4096]{1,0:T(8,128)} fusion(f32[768,4096]{1,0:T(8,128)} %fusion.116, f32[768,4096]{1,0:T(8,128)} %fusion.29, f32[768,4096]{1,0:T(8,128)} %fusion.33, bf16[4096,256]{1,0:T(8,128)(2,1)S(1)} %copy-done, f32[3,512]{0,1:T(8,128)S(1)} %add_add_fusion.1, f32[765,512]{0,1:T(8,128)} %copy-done.3), kind=kOutput, calls=%fused_computation.6 | convolution fusion | flops 9673310208 | bytes 54001664 | tf_op jit(solution)/shard_map/dot_general | solution.py:198
  448.0 175.6 %reduce-scatter.2.cloned.1.call-done = f32[24,4096]{1,0:T(8,128)} async-done(((f32[768,4096]{1,0:T(8,128)}), f32[24,4096]{1,0:T(8,128)}) %reduce-scatter.2.cloned.1.call-update) | async-done | bytes 393232 | tf_op jit(solution)/shard_map/reduce_scatter | solution.py:201
  623.6 1.7 convert_element_type.50
  (179 shorter events, 31.0 us)
Async XLA Ops:
  6.5 107.9 %copy-start = (bf16[4096,256]{1,0:T(8,128)(2,1)S(1)}, bf16[4096,256]{1,0:T(8,128)(2,1)}, u32[]{:S(2)}) copy-start(bf16[4096,256]{1,0:T(8,128)(2,1)} %param.18) | copy-start | bytes 6291460
  6.5 102.3 %all-gather.8.cloned.1.call-start = ((), (), s32[]{:S(2)}) async-start(), calls=%async_computation.1 | async-start | bytes 6488064 | tf_op jit(solution)/shard_map/all_gather | solution.py:109
  7.3 195.5 %all-gather.10.cloned.1.call-start = ((), (), s32[]{:S(2)}) async-start(), calls=%async_computation.2 | async-start | bytes 6488064 | tf_op jit(solution)/shard_map/all_gather | solution.py:110
  8.0 229.2 %all-gather.12.cloned.1.call-start = ((), (), s32[]{:S(2)}) async-start(), calls=%async_computation.4 | async-start | bytes 1179648 | tf_op jit(solution)/shard_map/all_gather | solution.py:25
  8.7 117.0 %copy-start.39 = (f32[2]{0:T(128)}, f32[2]{0:T(128)S(1)}, u32[]{:S(2)}) copy-start(f32[2]{0:T(128)S(1)} %exp.63) | copy-start | bytes 28
  10.1 118.4 %copy-start.29 = (f32[1,512]{1,0:T(1,128)}, f32[1,512]{1,0:T(1,128)S(1)}, u32[]{:S(2)}) copy-start(f32[1,512]{1,0:T(1,128)S(1)} %get-tuple-element.311) | copy-start | bytes 6148
  10.1 118.4 %copy-start.31 = (f32[1,512]{1,0:T(1,128)}, f32[1,512]{1,0:T(1,128)S(1)}, u32[]{:S(2)}) copy-start(f32[1,512]{1,0:T(1,128)S(1)} %get-tuple-element.313) | copy-start | bytes 6148
  10.1 118.4 %copy-start.33 = (f32[1,512]{1,0:T(1,128)}, f32[1,512]{1,0:T(1,128)S(1)}, u32[]{:S(2)}) copy-start(f32[1,512]{1,0:T(1,128)S(1)} %get-tuple-element.314) | copy-start | bytes 6148
  10.1 118.4 %copy-start.35 = (f32[1,512]{1,0:T(1,128)}, f32[1,512]{1,0:T(1,128)S(1)}, u32[]{:S(2)}) copy-start(f32[1,512]{1,0:T(1,128)S(1)} %get-tuple-element.312) | copy-start | bytes 6148
  113.4 226.3 %copy-start.42 = (f32[2,768]{1,0:T(2,128)}, f32[2,768]{1,0:T(2,128)S(1)}, u32[]{:S(2)}) copy-start(f32[2,768]{1,0:T(2,128)S(1)} %get-tuple-element.304) | copy-start | bytes 18436
  114.4 4.8 copy-start.5
  114.4 5.9 copy-start.7
  122.4 5.7 collective-permute-start
  125.7 5.5 copy-start.37
  125.9 5.3 copy-start.22
  131.2 2.8 copy-start.48
  133.8 236.4 %all-gather.14.cloned.1.call-start = ((), (), s32[]{:S(2)}) async-start(), calls=%async_computation.5 | async-start | bytes 1179648 | tf_op jit(solution)/shard_map/all_gather | solution.py:25
  202.8 6.4 %copy-start.2 = (f32[768,512]{0,1:T(8,128)S(1)}, f32[768,512]{0,1:T(8,128)}, u32[]{:S(2)}) copy-start(f32[768,512]{0,1:T(8,128)} %copy-done.1) | copy-start | bytes 4718596
  245.4 11.0 %copy-start.43 = (f32[8,2]{1,0:T(8,128)}, f32[8,2]{1,0:T(8,128)S(1)}, u32[]{:S(2)}) copy-start(f32[8,2]{1,0:T(8,128)S(1)} %get-tuple-element.457) | copy-start | bytes 196
  248.1 8.3 %copy-start.8 = (bf16[2,4096,256]{2,1,0:T(8,128)(2,1)S(1)}, bf16[2,4096,256]{2,1,0:T(8,128)(2,1)}, u32[]{:S(2)}) copy-start(bf16[2,4096,256]{2,1,0:T(8,128)(2,1)} %param.17) | copy-start | bytes 12582916
  248.1 8.3 %copy-start.12 = (f32[768,256]{0,1:T(8,128)S(1)}, f32[768,256]{0,1:T(8,128)}, u32[]{:S(2)}) copy-start(f32[768,256]{0,1:T(8,128)} %fusion.133) | copy-start | bytes 2359300
  248.1 8.3 %copy-start.45 = (f32[256]{0:T(256)S(1)}, f32[256]{0:T(256)}, u32[]{:S(2)}) copy-start(f32[256]{0:T(256)} %param.24) | copy-start | bytes 3076
  256.4 6.0 copy-start.14
  334.0 5.6 copy-start.23
  334.0 5.6 copy-start.25
  334.0 5.6 copy-start.27
  339.6 283.9 %reduce-scatter.2.cloned.1.call-start = ((), (), s32[]{:S(2)}) async-start(), calls=%async_computation.3 | async-start | bytes 12976128 | tf_op jit(solution)/shard_map/reduce_scatter | solution.py:201
  352.9 2.7 copy-start.19
  353.8 6.3 copy-start.16
  355.7 4.4 copy-start.13
  355.7 4.4 copy-start.15
  355.7 4.4 copy-start.24
  355.7 4.4 copy-start.26
  355.7 4.4 copy-start.28
  355.7 4.4 copy-start.46
  355.7 5.0 copy-start.9
  384.8 5.2 copy-start.47
  390.2 7.6 %copy-start.38 = (f32[2]{0:T(128)S(1)}, f32[2]{0:T(128)}, u32[]{:S(2)}) copy-start(f32[2]{0:T(128)} %copy-done.37) | copy-start | bytes 28
  390.2 10.9 %copy-start.17 = (f32[768,128]{0,1:T(8,128)S(1)}, f32[768,128]{0,1:T(8,128)}, u32[]{:S(2)}) copy-start(f32[768,128]{0,1:T(8,128)} %convolution_bitcast_fusion) | copy-start | bytes 1179652
  397.8 6.5 %copy-start.36 = (f32[1,512]{1,0:T(1,128)S(1)}, f32[1,512]{1,0:T(1,128)}, u32[]{:S(2)}) copy-start(f32[1,512]{1,0:T(1,128)} %copy-done.35) | copy-start | bytes 6148
  401.0 3.4 copy-start.6
  401.0 3.4 copy-start.18
  405.5 1.7 copy-start.20
  405.5 1.8 copy-start.21
  405.5 1.8 copy-start.40
  405.5 1.8 copy-start.41
  405.7 10.1 %collective-permute-start.1 = (f32[3,512]{0,1:T(8,128)S(1)}, f32[3,512]{0,1:T(8,128)S(1)}, u32[]{:S(2)}, u32[]{:S(2)}) collective-permute-start(f32[3,512]{0,1:T(8,128)S(1)} %pad_add_fusion.1), channel_id=1, source_target_pairs={{32,0},{64,32},{96,64},{128,96},{160,128},{192,160},{224,192},{33,... | collective-permute-start | bytes 18440 | tf_op jit(solution)/shard_map/ppermute | solution.py:20
  415.8 2.8 copy-start.10
  (8 other events, 7.9 us)
Sparse Core Ops, SparseCore 0:
  10.1 98.7 all-gather.7
  111.6 91.0 all-gather.9
  204.6 32.5 all-gather.11
  339.8 30.3 all-gather.13
  448.1 175.4 reduce-scatter.1
where the time goes:
time: 642 us; the launch traced here: 632 us
  waiting for transfers between devices  355 us (55%)
  matrix products  116 us (18%)
  blocking collectives  87.7 us (14%)
  other arithmetic  35.9 us (6%)
  local copies, waits for them, and re-layouts  16.9 us (3%)
  between operations  14.6 us (2%)
    reduce_scatter x1, waiting for transfers between devices, body(): lax.psum_scatter(summed_term, 'tp', scatter_dimension=0, tiled=True)  176 us
    all_gather x1, waiting for transfers between devices, body(): lax.all_gather(normed_rows, 'tp', axis=0, tiled=True)  98.7 us
    psum x1, blocking collectives, body(): lax.psum((jnp.sum(gated_out * gated_out, axis=1), jnp.sum(norm_gain * out...  71.5 us
    all_gather x1, waiting for transfers between devices, body(): lax.all_gather(out_grad, 'tp', axis=0, tiled=True)  49.8 us
    all_gather x2, waiting for transfers between devices, prefix(): everything = jax.tree.map(lambda part: lax.all_gather(part, axis), value)  27.7 us
    dot_general x3, matrix products, within_shard(): local_part = jnp.einsum('hts,shp->thp', weights, inner_act, precision=EXACT)  26.1 us
    dot_general x1, matrix products, body(): jnp.dot(d_state, state_float.T, precision=EXACT, preferred_element_type=j...  23 us
    unnamed x1, blocking collectives  16.2 us
  transfers between devices with their start and end apart: 7, of which 6 were waited for; matrix products, arithmetic and copies ran while one was open for 11% of the time, Pallas kernels for 0%

commit v1 on v0

v1 whole, which is shorter than its diff:
```python
import functools

import jax
import jax.numpy as jnp
from jax import lax
from jax.experimental import pallas as pl
from jax.experimental.pallas import tpu as pltpu
from jax.sharding import PartitionSpec as P

HEAD_DIM = 128
STATE = 128
CONV = 4
EPSILON = 1e-05
EXACT = lax.Precision.HIGHEST
MESH = pl.DeviceIdType.MESH
F32 = jnp.float32
BF16 = jnp.bfloat16
VMEM_LIMIT = 60 * 1024 * 1024

Z = 8
RING = [(0, 0), (0, 1), (1, 0), (1, 1), (2, 0), (2, 1)]


def place():
    tp = lax.axis_index("tp")
    core = lax.rem(tp, 2)
    z = lax.rem(tp // 2, Z)
    yh = tp // (2 * Z)
    return yh, z, core


def tp_id(yh, z, core):
    return (yh * Z + z) * 2 + core


def greet(tp_partners, ctx_partners=()):
    barrier = pltpu.get_barrier_semaphore()
    for partner in tp_partners:
        pl.semaphore_signal(barrier, inc=1, device_id={"tp": partner}, device_id_type=MESH)
    for partner in ctx_partners:
        pl.semaphore_signal(barrier, inc=1, device_id={"ctx": partner}, device_id_type=MESH)
    pl.semaphore_wait(barrier, len(tp_partners) + len(ctx_partners))


class Gather:
    def __init__(self, own_ref, buf, swap, send_sem, recv_sem):
        self.own_ref, self.buf, self.swap = own_ref, buf, swap
        self.send_sem, self.recv_sem = send_sem, recv_sem
        self.yh, self.z, self.core = place()
        self.pair = 2 * own_ref.shape[0]
        self.half = own_ref.shape[1] // 2
        self.sibling = tp_id(self.yh, self.z, 1 - self.core)
        self.started = []

    def columns(self, core):
        return pl.ds(pl.multiple_of(core * self.half, self.half), self.half)

    def block(self, h, dz, core=None):
        yh = self.yh if h == 0 else 1 - self.yh
        chip = yh * Z + lax.rem(self.z + (dz + Z), Z)
        rows = pl.ds(pl.multiple_of(chip * self.pair, 16), self.pair)
        return self.buf.at[rows, self.columns(self.core if core is None else core)]

    def copy(self, slot, src, dst, partner):
        return pltpu.make_async_remote_copy(
            src_ref=src,
            dst_ref=dst,
            send_sem=self.send_sem.at[slot],
            recv_sem=self.recv_sem.at[slot],
            device_id={"tp": partner},
            device_id_type=MESH,
        )

    def send(self, slot, src, dst, partner):
        copy = self.copy(slot, src, dst, partner)
        copy.start()
        self.started.append(copy)

    def slot(self, way, s, h):
        return (1 if way > 0 else 8) + (2 * s + h if s < 3 else 6)

    def sibling_slot(self, h, dz):
        return 15 + (dz + 3) * 2 + h if dz > -4 else 15 + (14 if h == 0 else 15)

    def to_sibling(self, h, dz):
        here = self.block(h, dz)
        self.send(self.sibling_slot(h, dz), here, here, self.sibling)

    def along(self, way, s, h):
        here = self.block(h, -way * s)
        partner = tp_id(self.yh, lax.rem(self.z + way + Z, Z), self.core)
        self.send(self.slot(way, s, h), here, here, partner)

    def first_swap(self):
        self.send(31, self.own_ref.at[:, self.columns(1 - self.core)], self.swap, self.sibling)

    def begin(self):
        self.got(31, self.swap)
        mine = self.own_ref[:, self.columns(self.core)].astype(F32)
        other = self.swap[...].astype(F32)
        first = self.core == 0
        both = jnp.concatenate([jnp.where(first, mine, other), jnp.where(first, other, mine)], axis=0)
        here = self.block(0, 0)
        here[...] = both.astype(BF16)
        self.send(0, here, here, tp_id(1 - self.yh, self.z, self.core))
        self.along(1, 0, 0)
        self.along(-1, 0, 0)
        self.to_sibling(0, 0)

    def got(self, slot, block):
        self.copy(slot, block, block, self.sibling).wait_recv()

    def across(self):
        self.got(0, self.block(1, 0))
        self.along(1, 0, 1)
        self.along(-1, 0, 1)
        self.to_sibling(1, 0)

    def ring(self, s, h):
        for way in (1, -1):
            dz = -way * (s + 1)
            self.got(self.slot(way, s, h), self.block(h, dz))
            if s < 2 or (way > 0) == (h == 0):
                self.along(way, s + 1, h)
            self.to_sibling(h, dz)

    def last(self):
        for way, h in ((1, 0), (-1, 1)):
            self.got(self.slot(way, 3, h), self.block(h, -4))
            self.to_sibling(h, -4)

    def finish(self):
        for h in (0, 1):
            for dz in range(-4, 4):
                self.got(self.sibling_slot(h, dz), self.block(h, dz, 1 - self.core))

    def drain(self):
        for copy in self.started:
            copy.wait_send()

    def steps(self):
        return (
            [self.begin, self.across]
            + [functools.partial(self.ring, s, h) for s, h in RING]
            + [self.last]
        )


def gather_kernel(
    rows_ref,
    grads_ref,
    inner_hbm,
    state_hbm,
    step_ref,
    out_hbm,
    gate_ref,
    conv_ref,
    stepraw_ref,
    local_ref,
    rows_all,
    grads_all,
    swaps,
    inner_w,
    state_w,
    out_w,
    send_r,
    recv_r,
    send_g,
    recv_g,
    weight_sem,
):
    loads = [
        pltpu.make_async_copy(inner_hbm, inner_w, weight_sem.at[0]),
        pltpu.make_async_copy(state_hbm, state_w, weight_sem.at[1]),
        pltpu.make_async_copy(out_hbm, out_w, weight_sem.at[2]),
    ]
    for load in loads:
        load.start()
    yh, z, core = place()
    greet(
        [
            tp_id(1 - yh, z, core),
            tp_id(yh, lax.rem(z + 1, Z), core),
            tp_id(yh, lax.rem(z + Z - 1, Z), core),
            tp_id(yh, z, 1 - core),
        ]
    )
    first = Gather(rows_ref, rows_all, swaps.at[0], send_r, recv_r)
    second = Gather(grads_ref, grads_all, swaps.at[1], send_g, recv_g)
    first.first_swap()
    second.first_swap()
    for step in first.steps()[:-1]:
        step()
    second.begin()
    first.last()
    second.across()
    for load in loads:
        load.wait()
    first.finish()
    total = rows_all.shape[0]
    tile = 128

    def project(dst, column, weight):
        def turn(i, carry):
            at = pl.ds(pl.multiple_of(i * tile, tile), tile)
            value = jnp.dot(rows_all[at, :], weight[...], preferred_element_type=F32)
            dst[at, pl.ds(column, value.shape[1])] = value.astype(BF16).astype(dst.dtype)
            return carry

        lax.fori_loop(0, total // tile, turn, 0)

    width = inner_w.shape[2]
    work = [
        lambda: project(conv_ref, 0, inner_w.at[1]),
        lambda: project(conv_ref, width, state_w),
        lambda: project(stepraw_ref, 0, step_ref),
        lambda: project(gate_ref, 0, inner_w.at[0]),
    ]
    pending = [functools.partial(second.ring, s, h) for s, h in RING] + [second.last]
    for at, step in enumerate(pending):
        step()
        if at < len(work):
            work[at]()
    second.finish()

    def turn(i, carry):
        at = pl.ds(pl.multiple_of(i * tile, tile), tile)
        local_ref[at, :] = lax.dot_general(
            grads_all[at, :], out_w[...], (((1,), (1,)), ((), ())), preferred_element_type=F32
        )
        return carry

    lax.fori_loop(0, total // tile, turn, 0)
    first.drain()
    second.drain()


def gathered(rows, grads, inner_weight, state_weight, step_weight, out_weight):
    count, depth = rows.shape
    total = count * 4 * Z
    width, state_width = inner_weight.shape[2], state_weight.shape[1]
    vmem = pl.BlockSpec(memory_space=pltpu.VMEM)
    anywhere = pl.BlockSpec(memory_space=pl.ANY)
    return pl.pallas_call(
        gather_kernel,
        out_shape=(
            jax.ShapeDtypeStruct((total, width), BF16),
            jax.ShapeDtypeStruct((total, width + state_width), BF16),
            jax.ShapeDtypeStruct((total, 128), F32),
            jax.ShapeDtypeStruct((total, width), F32),
        ),
        in_specs=[vmem, vmem, anywhere, anywhere, vmem, anywhere],
        out_specs=(vmem, vmem, vmem, vmem),
        scratch_shapes=[
            pltpu.VMEM((total, depth), BF16),
            pltpu.VMEM((total, depth), BF16),
            pltpu.VMEM((2, count, depth // 2), BF16),
            pltpu.VMEM(inner_weight.shape, BF16),
            pltpu.VMEM(state_weight.shape, BF16),
            pltpu.VMEM(out_weight.shape, BF16),
            pltpu.SemaphoreType.DMA((32,)),
            pltpu.SemaphoreType.DMA((32,)),
            pltpu.SemaphoreType.DMA((32,)),
            pltpu.SemaphoreType.DMA((32,)),
            pltpu.SemaphoreType.DMA((3,)),
        ],
        compiler_params=pltpu.CompilerParams(
            collective_id=0, has_side_effects=True, vmem_limit_bytes=VMEM_LIMIT
        ),
        name="gather_project",
    )(rows, grads, inner_weight, state_weight, step_weight, out_weight)


def scatter_kernel(
    gate_ref,
    inner_ref,
    dstate_ref,
    dstep_ref,
    inner_hbm,
    state_hbm,
    step_ref,
    out_ref,
    inner_w,
    state_w,
    mine,
    sib_out,
    sib_in,
    plus_out,
    plus_in,
    minus_out,
    minus_in,
    y_out,
    y_in,
    last_out,
    last_in,
    send_sib,
    recv_sib,
    send_ring,
    recv_ring,
    y_sem,
    weight_sem,
):
    loads = [
        pltpu.make_async_copy(inner_hbm, inner_w, weight_sem.at[0]),
        pltpu.make_async_copy(state_hbm, state_w, weight_sem.at[1]),
    ]
    for load in loads:
        load.start()
    yh, z, core = place()
    sibling = tp_id(yh, z, 1 - core)
    right = tp_id(yh, lax.rem(z + 1, Z), core)
    left = tp_id(yh, lax.rem(z + Z - 1, Z), core)
    across = tp_id(1 - yh, z, core)
    greet([across, right, left, sibling])
    for load in loads:
        load.wait()
    rows, depth = out_ref.shape
    pair, half = 2 * rows, depth // 2
    tile = 512
    started = []

    def remote(src, dst, send_sem, recv_sem, partner):
        return pltpu.make_async_remote_copy(
            src_ref=src,
            dst_ref=dst,
            send_sem=send_sem,
            recv_sem=recv_sem,
            device_id={"tp": partner},
            device_id_type=MESH,
        )

    dims = (((1,), (1,)), ((), ()))

    def product(place_at, dz):
        zt = lax.rem(z + (dz + Z), Z)
        spots = []
        for h in (0, 1):
            yt = yh if h == 0 else 1 - yh
            spots.append(pl.ds(pl.multiple_of((yt * Z + zt) * pair, 16), pair))

        def side(which, keep):
            def turn(j, carry):
                at = pl.ds(pl.multiple_of(j * tile, tile), tile)
                cols = pl.ds(pl.multiple_of(which * half + j * tile, tile), tile)
                parts = []
                for ref in (gate_ref, inner_ref, dstate_ref, dstep_ref):
                    parts.append(jnp.concatenate([ref[spots[0], :], ref[spots[1], :]], axis=0))
                value = lax.dot_general(parts[0], inner_w[0, cols, :], dims, preferred_element_type=F32)
                value += lax.dot_general(parts[1], inner_w[1, cols, :], dims, preferred_element_type=F32)
                value += lax.dot_general(parts[2], state_w[cols, :], dims, preferred_element_type=F32)
                value += lax.dot_general(parts[3], step_ref[cols, :], dims, preferred_element_type=F32)
                for h in (0, 1):
                    keep[place_at, h, :, at] = value[h * pair : (h + 1) * pair].astype(keep.dtype)
                return carry

            lax.fori_loop(0, half // tile, turn, 0)

        side(1 - core, sib_out)
        copy = remote(
            sib_out.at[place_at], sib_in.at[place_at], send_sib.at[place_at], recv_sib.at[place_at], sibling
        )
        copy.start()
        started.append(copy)
        side(core, mine)

    order = [-4, 3, -3, 2, -2, 1, -1, 0]
    places = {dz: i for i, dz in enumerate(order)}

    def ring_slot(way, d, h):
        base = 0 if way > 0 else 7
        return base + (0 if d == 4 else 1 + (3 - d) * 2 + (1 - h))

    def message(way, d, h):
        dz = way * d if d < 4 else -4
        at = places[dz]
        outs, ins = (plus_out, plus_in) if way > 0 else (minus_out, minus_in)
        slot = ring_slot(way, d, h)
        local = slot % 7
        earlier = None
        if d < 3 or (d == 3 and (way > 0) == (h == 0)):
            earlier = ring_slot(way, d + 1, h)
            before = ins.at[earlier % 7]
            remote(before, before, send_ring.at[earlier], recv_ring.at[earlier], right).wait_recv()

        def turn(j, carry):
            cols = pl.ds(pl.multiple_of(j * tile, tile), tile)
            value = mine[at, h, :, cols] + sib_in[at, h, :, cols].astype(F32)
            if earlier is not None:
                value += ins[earlier % 7, :, cols].astype(F32)
            outs[local, :, cols] = value.astype(BF16)
            return carry

        lax.fori_loop(0, half // tile, turn, 0)
        copy = remote(
            outs.at[local], ins.at[local], send_ring.at[slot], recv_ring.at[slot], right if way > 0 else left
        )
        copy.start()
        started.append(copy)

    def sib_got(dz):
        at = places[dz]
        there = sib_in.at[at]
        remote(there, there, send_sib.at[at], recv_sib.at[at], sibling).wait_recv()

    product(places[-4], -4)
    product(places[3], 3)
    sib_got(-4)
    message(1, 4, 0)
    message(-1, 4, 1)
    product(places[-3], -3)
    for d in (3, 2, 1):
        sib_got(d)
        message(1, d, 1 if d == 3 else 1)
        if d > 1:
            product(places[d - 1], d - 1)
        else:
            product(places[0], 0)
        sib_got(-d)
        message(-1, d, 1 if d < 3 else 0)
        message(1, d, 0)
        message(-1, d, 0 if d < 3 else 1)
        if d > 1:
            product(places[-(d - 1)], -(d - 1))
    sib_got(0)
    at = places[0]

    def ring_got(way, h):
        ins = plus_in if way > 0 else minus_in
        slot = ring_slot(way, 1, h)
        there = ins.at[slot % 7]
        remote(there, there, send_ring.at[slot], recv_ring.at[slot], right).wait_recv()
        return ins, slot % 7

    plus_ref, plus_at = ring_got(1, 1)
    minus_ref, minus_at = ring_got(-1, 1)

    def other(j, carry):
        cols = pl.ds(pl.multiple_of(j * tile, tile), tile)
        value = mine[at, 1, :, cols] + sib_in[at, 1, :, cols].astype(F32)
        value += plus_ref[plus_at, :, cols].astype(F32) + minus_ref[minus_at, :, cols].astype(F32)
        y_out[:, cols] = value.astype(BF16)
        return carry

    lax.fori_loop(0, half // tile, other, 0)
    swap = remote(y_out, y_in, y_sem.at[0], y_sem.at[1], across)
    swap.start()
    plus_own, plus_own_at = ring_got(1, 0)
    minus_own, minus_own_at = ring_got(-1, 0)
    swap.wait()

    first = core == 0

    def final(j, carry):
        cols = pl.ds(pl.multiple_of(j * tile, tile), tile)
        value = mine[at, 0, :, cols] + sib_in[at, 0, :, cols].astype(F32)
        value += plus_own[plus_own_at, :, cols].astype(F32) + minus_own[minus_own_at, :, cols].astype(F32)
        value += y_in[:, cols].astype(F32)
        low, high = value[:rows], value[rows:]
        here = pl.ds(pl.multiple_of(core * half + j * tile, tile), tile)
        out_ref[:, here] = jnp.where(first, low, high).astype(BF16)
        last_out[:, cols] = jnp.where(first, high, low).astype(BF16)
        return carry

    lax.fori_loop(0, half // tile, final, 0)
    swap = remote(last_out, last_in, y_sem.at[2], y_sem.at[3], sibling)
    swap.start()
    swap.wait()
    out_ref[:, pl.ds(pl.multiple_of((1 - core) * half, half), half)] = last_in[...]
    for copy in started:
        copy.wait_send()


def scattered(d_gate, d_inner, d_state, d_step, inner_weight, state_weight, step_weight):
    total = d_gate.shape[0]
    rows, depth = total // (4 * Z), state_weight.shape[0]
    vmem = pl.BlockSpec(memory_space=pltpu.VMEM)
    anywhere = pl.BlockSpec(memory_space=pl.ANY)
    return pl.pallas_call(
        scatter_kernel,
        out_shape=jax.ShapeDtypeStruct((rows, depth), BF16),
        in_specs=[vmem, vmem, vmem, vmem, anywhere, anywhere, vmem],
        out_specs=vmem,
        scratch_shapes=[
            pltpu.VMEM(inner_weight.shape, BF16),
            pltpu.VMEM(state_weight.shape, BF16),
            pltpu.VMEM((Z, 2, 2 * rows, depth // 2), F32),
            pltpu.VMEM((Z, 2, 2 * rows, depth // 2), BF16),
            pltpu.VMEM((Z, 2, 2 * rows, depth // 2), BF16),
            pltpu.VMEM((7, 2 * rows, depth // 2), BF16),
            pltpu.VMEM((7, 2 * rows, depth // 2), BF16),
            pltpu.VMEM((7, 2 * rows, depth // 2), BF16),
            pltpu.VMEM((7, 2 * rows, depth // 2), BF16),
            pltpu.VMEM((2 * rows, depth // 2), BF16),
            pltpu.VMEM((2 * rows, depth // 2), BF16),
            pltpu.VMEM((rows, depth // 2), BF16),
            pltpu.VMEM((rows, depth // 2), BF16),
            pltpu.SemaphoreType.DMA((Z,)),
            pltpu.SemaphoreType.DMA((Z,)),
            pltpu.SemaphoreType.DMA((14,)),
            pltpu.SemaphoreType.DMA((14,)),
            pltpu.SemaphoreType.DMA((4,)),
            pltpu.SemaphoreType.DMA((2,)),
        ],
        compiler_params=pltpu.CompilerParams(
            collective_id=1, has_side_effects=True, vmem_limit_bytes=VMEM_LIMIT
        ),
        name="product_scatter",
    )(d_gate, d_inner, d_state, d_step, inner_weight, state_weight, step_weight)


def to(axis, partner, src, dst, send_sem, recv_sem):
    return pltpu.make_async_remote_copy(
        src_ref=src,
        dst_ref=dst,
        send_sem=send_sem,
        recv_sem=recv_sem,
        device_id={axis: partner},
        device_id_type=MESH,
    )


def dot(a, b, contract, precision=EXACT):
    return lax.dot_general(
        a, b, (contract, ((), ())), precision=precision, preferred_element_type=F32
    )


NN, NT, TN = ((1,), (0,)), ((1,), (1,)), ((0,), (0,))
CHUNK = 128
HALO = 8
SHARDS = 8


def mixer_kernel(
    step_bias_ref,
    decay_log_ref,
    gate_ref,
    conv_ref,
    stepraw_ref,
    local_ref,
    conv_inner_ref,
    conv_state_ref,
    gain_ref,
    d_gate_ref,
    d_inner_ref,
    d_state_ref,
    d_step_ref,
    ext,
    pre,
    act,
    xd,
    steps,
    cums,
    cb,
    decays,
    out,
    dy,
    states,
    d_states,
    entering,
    d_leaving,
    fwd_out,
    fwd_in,
    bwd_out,
    bwd_in,
    tot_out,
    tot_in,
    d_pre,
    d_b,
    u_loc,
    halo_sem,
    fwd_send,
    fwd_recv,
    bwd_send,
    bwd_recv,
    tot_send,
    tot_recv,
):
    tp, ctx = lax.axis_index("tp"), lax.axis_index("ctx")
    group = 4 * Z
    barrier = pltpu.get_barrier_semaphore()
    for j in range(1, group):
        pl.semaphore_signal(barrier, inc=1, device_id={"tp": lax.rem(tp + j, group)}, device_id_type=MESH)
    for j in range(1, SHARDS):
        pl.semaphore_signal(barrier, inc=1, device_id={"ctx": lax.rem(ctx + j, SHARDS)}, device_id_type=MESH)
    total = conv_ref.shape[0]
    width = gate_ref.shape[1]
    heads = width // HEAD_DIM
    chunks = total // CHUNK
    channels = width * group
    span = lambda k: slice(k * CHUNK, (k + 1) * CHUNK)
    ext[HALO:, :] = conv_ref[...].astype(F32)
    pl.semaphore_wait(barrier, group + SHARDS - 2)

    halo = to("ctx", lax.rem(ctx + 1, SHARDS), ext.at[total:, :], ext.at[:HALO, :], halo_sem.at[0], halo_sem.at[1])

    @pl.when(ctx < SHARDS - 1)
    def _():
        halo.start()

    lane = lax.broadcasted_iota(jnp.int32, (1, CHUNK), 1)
    rows_at = lax.broadcasted_iota(jnp.int32, (CHUNK, CHUNK), 0)
    cols_at = lax.broadcasted_iota(jnp.int32, (CHUNK, CHUNK), 1)
    causal = (rows_at >= cols_at).astype(F32)
    anti = (rows_at <= cols_at).astype(F32)

    def per_lane(values):
        row = jnp.zeros_like(values[0])
        for h, value in enumerate(values):
            row = jnp.where(lane == h, value, row)
        return row

    bias = per_lane([jnp.full((1, CHUNK), step_bias_ref[h], F32) for h in range(heads)])
    rate = per_lane([jnp.exp(jnp.full((1, CHUNK), decay_log_ref[h], F32)) for h in range(heads)])
    valid = lane < heads
    kernel = [
        jnp.concatenate([conv_inner_ref[k : k + 1, :], conv_state_ref[k : k + 1, :]], axis=1)
        for k in range(CONV)
    ]

    ends = []
    for k in range(chunks):
        raw = jnp.where(valid, stepraw_ref[span(k), :], 0.0) + bias
        step = jnp.maximum(raw, 0.0) + jnp.log1p(jnp.exp(-jnp.abs(raw)))
        step = jnp.where(valid, step, 0.0)
        steps[span(k), :] = step
        cum = dot(causal, -step * rate, NN)
        cums[span(k), :] = cum
        turned = cum.T
        ends.append([cum[CHUNK - 1 :, h : h + 1] for h in range(heads)])
        for h in range(heads):
            spread = cum[:, h : h + 1] - turned[h : h + 1, :]
            decays[k, h] = jnp.exp(jnp.minimum(spread, 0.0)) * causal

    @pl.when(ctx == 0)
    def _():
        ext[:HALO, :] = jnp.zeros((HALO, ext.shape[1]), F32)

    @pl.when(ctx > 0)
    def _():
        halo.wait_recv()

    for k in range(chunks):
        blended = jnp.zeros((CHUNK, ext.shape[1]), F32)
        for tap in range(CONV):
            start = k * CHUNK + HALO - (CONV - 1) + tap
            blended += kernel[tap] * ext[start : start + CHUNK, :]
        pre[span(k), :] = blended
        active = blended * jax.nn.sigmoid(blended)
        act[span(k), :] = active
        b_rows, c_rows = active[:, width : width + STATE], active[:, width + STATE :]
        cb[k] = dot(c_rows, b_rows, NT)
        for h in range(heads):
            lanes = slice(h * HEAD_DIM, (h + 1) * HEAD_DIM)
            fed = active[:, lanes] * steps[span(k), h : h + 1]
            xd[span(k), lanes] = fed
            left = jnp.exp(ends[k][h] - cums[span(k), h : h + 1])
            own = dot(fed * left, b_rows, TN)
            if k == 0:
                states[0, h] = jnp.zeros_like(own)
                states[1, h] = own
            else:
                states[k + 1, h] = jnp.exp(ends[k][h]) * states[k, h] + own

    befores = [[jnp.zeros((1, 1), F32) for _ in range(heads)]]
    for k in range(chunks):
        befores.append([befores[k][h] + ends[k][h] for h in range(heads)])
    whole = [jnp.exp(befores[chunks][h]) for h in range(heads)]
    row8 = lax.broadcasted_iota(jnp.int32, (8, CHUNK), 0)
    factors = jnp.zeros((8, CHUNK), F32)
    for h in range(heads):
        fwd_out[h * HEAD_DIM : (h + 1) * HEAD_DIM, :] = states[chunks, h]
        factors = jnp.where(row8 == h, whole[h], factors)
    fwd_out[heads * HEAD_DIM :, :] = factors
    bwd_out[heads * HEAD_DIM :, :] = factors

    forward = []
    for d in range(1, SHARDS):
        copy = to("ctx", lax.rem(ctx + d, SHARDS), fwd_out, fwd_in.at[d - 1], fwd_send.at[d - 1], fwd_recv.at[d - 1])
        forward.append(copy)

        @pl.when(ctx + d < SHARDS)
        def _(copy=copy):
            copy.start()

    def collect(gathered_in, copies, into, there):
        into[...] = jnp.zeros_like(into)
        for d in range(SHARDS - 1, 0, -1):

            @pl.when(there(d))
            def _(d=d):
                copies[d - 1].wait_recv()
                for h in range(heads):
                    at = heads * HEAD_DIM + h
                    factor = gathered_in[d - 1, at : at + 1, :]
                    into[h] = into[h] * factor + gathered_in[d - 1, h * HEAD_DIM : (h + 1) * HEAD_DIM, :]

    for k in range(chunks):
        c_rows = act[span(k), width + STATE :]
        for h in range(heads):
            lanes = slice(h * HEAD_DIM, (h + 1) * HEAD_DIM)
            value = dot(decays[k, h] * cb[k], xd[span(k), lanes], NN)
            if k > 0:
                value += jnp.exp(cums[span(k), h : h + 1]) * dot(c_rows, states[k, h], NT)
            out[span(k), lanes] = value

    collect(fwd_in, forward, entering, lambda d: ctx >= d)
    gain = gain_ref[...]
    ones = jnp.ones((8, width), F32)
    for k in range(chunks):
        c_rows = act[span(k), width + STATE :]
        for h in range(heads):
            lanes = slice(h * HEAD_DIM, (h + 1) * HEAD_DIM)
            grown = jnp.exp(cums[span(k), h : h + 1] + befores[k][h])
            out[span(k), lanes] = out[span(k), lanes] + grown * dot(c_rows, entering[h], NT)
            states[k, h] = states[k, h] + jnp.exp(befores[k][h]) * entering[h]
        gate = gate_ref[span(k), :].astype(F32)
        gated = out[span(k), :] * (gate * jax.nn.sigmoid(gate))
        squares = dot(ones, gated * gated, NT)
        crosses = dot(ones, gain * local_ref[span(k), :] * gated, NT)
        tot_out[0:1, span(k)] = squares[0:1, :]
        tot_out[1:2, span(k)] = crosses[0:1, :]
    for h in range(heads):
        states[chunks, h] = states[chunks, h] + whole[h] * entering[h]

    totals = []
    for j in range(1, group):
        copy = to("tp", lax.rem(tp + j, group), tot_out, tot_in.at[j - 1], tot_send.at[j - 1], tot_recv.at[j - 1])
        copy.start()
        totals.append(copy)
    sums = tot_out[...]
    for j, copy in enumerate(totals):
        copy.wait_recv()
        sums = sums + tot_in[j]

    for k in range(chunks):
        held = jnp.concatenate([sums[:, span(k)], jnp.zeros((CHUNK - 2, CHUNK), F32)], axis=0).T
        inverse = lax.rsqrt(held[:, 0:1] / channels + EPSILON)
        pull = inverse * inverse * inverse * (held[:, 1:2] / channels)
        gate = gate_ref[span(k), :].astype(F32)
        sigmoid = jax.nn.sigmoid(gate)
        opened = gate * sigmoid
        value = out[span(k), :]
        d_gated = inverse * (gain * local_ref[span(k), :]) - value * opened * pull
        d_gate_ref[span(k), :] = (d_gated * value * sigmoid * (1.0 + gate * (1.0 - sigmoid))).astype(BF16)
        dy[span(k), :] = d_gated * opened

    for k in range(chunks - 1, -1, -1):
        c_rows = act[span(k), width + STATE :]
        for h in range(heads):
            lanes = slice(h * HEAD_DIM, (h + 1) * HEAD_DIM)
            own = dot(dy[span(k), lanes] * jnp.exp(cums[span(k), h : h + 1]), c_rows, TN)
            if k < chunks - 1:
                own += jnp.exp(ends[k][h]) * d_states[k + 1, h]
            d_states[k, h] = own
    for h in range(heads):
        bwd_out[h * HEAD_DIM : (h + 1) * HEAD_DIM, :] = d_states[0, h]
    backward = []
    for d in range(1, SHARDS):
        copy = to("ctx", lax.rem(ctx + SHARDS - d, SHARDS), bwd_out, bwd_in.at[d - 1], bwd_send.at[d - 1], bwd_recv.at[d - 1])
        backward.append(copy)

        @pl.when(ctx >= d)
        def _(copy=copy):
            copy.start()

    d_c = cb
    for k in range(chunks):
        b_rows, c_rows = act[span(k), width : width + STATE], act[span(k), width + STATE :]
        d_cb = jnp.zeros((CHUNK, CHUNK), F32)
        d_crows = jnp.zeros((CHUNK, STATE), F32)
        for h in range(heads):
            lanes = slice(h * HEAD_DIM, (h + 1) * HEAD_DIM)
            grad = dy[span(k), lanes]
            d_cb += decays[k, h] * dot(grad, xd[span(k), lanes], NT)
            u_loc[span(k), lanes] = dot(decays[k, h] * cb[k], grad, TN)
            d_crows += jnp.exp(cums[span(k), h : h + 1]) * dot(grad, states[k, h], NN)
        d_b[span(k), :] = dot(d_cb, c_rows, TN)
        d_c[k] = d_crows + dot(d_cb, b_rows, NN)

    collect(bwd_in, backward, d_leaving, lambda d: ctx + d < SHARDS)
    after = [jnp.zeros((1, 1), F32) for _ in range(heads)]
    d_states[chunks] = d_leaving[...]
    for k in range(chunks - 1, 0, -1):
        after = [after[h] + ends[k][h] for h in range(heads)]
        for h in range(heads):
            d_states[k, h] = d_states[k, h] + jnp.exp(after[h]) * d_leaving[h]

    halo2 = to("ctx", lax.rem(ctx + SHARDS - 1, SHARDS), d_pre.at[:HALO, :], d_pre.at[total:, :], halo_sem.at[2], halo_sem.at[3])
    for k in range(chunks):
        b_rows = act[span(k), width : width + STATE]
        d_brows = d_b[span(k), :]
        d_acts = []
        pulls = jnp.zeros((CHUNK, CHUNK), F32)
        feeds = jnp.zeros((CHUNK, CHUNK), F32)
        edge = jnp.zeros((1, CHUNK), F32)
        for h in range(heads):
            lanes = slice(h * HEAD_DIM, (h + 1) * HEAD_DIM)
            step = steps[span(k), h : h + 1]
            left = jnp.exp(ends[k][h] - cums[span(k), h : h + 1])
            d_next = d_states[k + 1, h]
            grad = u_loc[span(k), lanes] + left * dot(b_rows, d_next, NT)
            d_brows += dot(xd[span(k), lanes] * left, d_next, NN)
            d_acts.append(grad * step)
            fed = jnp.sum(grad * act[span(k), lanes], axis=1, keepdims=True)
            met = jnp.sum(dy[span(k), lanes] * out[span(k), lanes], axis=1, keepdims=True)
            pulls = jnp.where(lane == h, met - step * fed, pulls)
            feeds = jnp.where(lane == h, fed, feeds)
            edge = jnp.where(lane == h, jnp.sum(d_next * states[k + 1, h]), edge)
        d_decay = dot(anti, pulls, NN) + edge
        raw = jnp.where(valid, stepraw_ref[span(k), :], 0.0) + bias
        d_raw = (feeds - rate * d_decay) * jax.nn.sigmoid(raw)
        d_step_ref[span(k), :] = d_raw[:, :heads].astype(BF16)
        d_act = jnp.concatenate(d_acts + [d_brows, d_c[k]], axis=1)
        value = pre[span(k), :]
        sigmoid = jax.nn.sigmoid(value)
        d_pre[span(k), :] = d_act * sigmoid * (1.0 + value * (1.0 - sigmoid))
        if k == 0:

            @pl.when(ctx > 0)
            def _():
                halo2.start()

    @pl.when(ctx == SHARDS - 1)
    def _():
        d_pre[total:, :] = jnp.zeros((HALO, d_pre.shape[1]), F32)

    @pl.when(ctx < SHARDS - 1)
    def _():
        halo2.wait_recv()

    for k in range(chunks):
        blended = jnp.zeros((CHUNK, ext.shape[1]), F32)
        for tap in range(CONV):
            start = k * CHUNK + CONV - 1 - tap
            blended += kernel[tap] * d_pre[start : start + CHUNK, :]
        d_inner_ref[span(k), :] = blended[:, :width].astype(BF16)
        d_state_ref[span(k), :] = blended[:, width:].astype(BF16)

    @pl.when(ctx < SHARDS - 1)
    def _():
        halo.wait_send()

    @pl.when(ctx > 0)
    def _():
        halo2.wait_send()

    for d in range(1, SHARDS):

        @pl.when(ctx + d < SHARDS)
        def _(d=d):
            forward[d - 1].wait_send()

        @pl.when(ctx >= d)
        def _(d=d):
            backward[d - 1].wait_send()

    for copy in totals:
        copy.wait_send()


def mixed(gate, conv, stepraw, local, conv_inner, conv_state, step_bias, decay_log, norm_gain):
    total, width = gate.shape
    heads = width // HEAD_DIM
    both = conv.shape[1]
    chunks = total // CHUNK
    group = 4 * Z
    vmem = pl.BlockSpec(memory_space=pltpu.VMEM)
    smem = pl.BlockSpec(memory_space=pltpu.SMEM)
    message = heads * HEAD_DIM + 8
    return pl.pallas_call(
        mixer_kernel,
        out_shape=(
            jax.ShapeDtypeStruct((total, width), BF16),
            jax.ShapeDtypeStruct((total, width), BF16),
            jax.ShapeDtypeStruct((total, both - width), BF16),
            jax.ShapeDtypeStruct((total, heads), BF16),
        ),
        in_specs=[smem, smem] + [vmem] * 7,
        out_specs=(vmem,) * 4,
        scratch_shapes=[
            pltpu.VMEM((HALO + total, both), F32),
            pltpu.VMEM((total, both), F32),
            pltpu.VMEM((total, both), F32),
            pltpu.VMEM((total, width), F32),
            pltpu.VMEM((total, CHUNK), F32),
            pltpu.VMEM((total, CHUNK), F32),
            pltpu.VMEM((chunks, CHUNK, CHUNK), F32),
            pltpu.VMEM((chunks, heads, CHUNK, CHUNK), F32),
            pltpu.VMEM((total, width), F32),
            pltpu.VMEM((total, width), F32),
            pltpu.VMEM((chunks + 1, heads, HEAD_DIM, STATE), F32),
            pltpu.VMEM((chunks + 1, heads, HEAD_DIM, STATE), F32),
            pltpu.VMEM((heads, HEAD_DIM, STATE), F32),
            pltpu.VMEM((heads, HEAD_DIM, STATE), F32),
            pltpu.VMEM((message, STATE), F32),
            pltpu.VMEM((SHARDS - 1, message, STATE), F32),
            pltpu.VMEM((message, STATE), F32),
            pltpu.VMEM((SHARDS - 1, message, STATE), F32),
            pltpu.VMEM((2, total), F32),
            pltpu.VMEM((group - 1, 2, total), F32),
            pltpu.VMEM((total + HALO, both), F32),
            pltpu.VMEM((total, STATE), F32),
            pltpu.VMEM((total, width), F32),
            pltpu.SemaphoreType.DMA((4,)),
            pltpu.SemaphoreType.DMA((SHARDS - 1,)),
            pltpu.SemaphoreType.DMA((SHARDS - 1,)),
            pltpu.SemaphoreType.DMA((SHARDS - 1,)),
            pltpu.SemaphoreType.DMA((SHARDS - 1,)),
            pltpu.SemaphoreType.DMA((group - 1,)),
            pltpu.SemaphoreType.DMA((group - 1,)),
        ],
        compiler_params=pltpu.CompilerParams(
            collective_id=2, has_side_effects=True, vmem_limit_bytes=VMEM_LIMIT
        ),
        name="mixer",
    )(step_bias, decay_log, gate, conv, stepraw, local, conv_inner, conv_state, norm_gain.reshape(1, -1))


def body(
    normed_rows,
    out_grad,
    inner_weight,
    state_weight,
    step_weight,
    conv_inner,
    conv_state,
    step_bias,
    decay_log,
    norm_gain,
    out_weight,
):
    gate, conv, stepraw, local = gathered(
        normed_rows, out_grad, inner_weight, state_weight, step_weight, out_weight
    )
    d_gate, d_inner, d_state, d_step = mixed(
        gate, conv, stepraw, local, conv_inner, conv_state, step_bias, decay_log, norm_gain
    )
    return scattered(d_gate, d_inner, d_state, d_step, inner_weight, state_weight, step_weight)


def solution(mesh):
    placed = (
        P(("ctx", "tp"), None),
        P(("ctx", "tp"), None),
        P(None, None, "tp"),
        P(),
        P(None, "tp"),
        P(None, "tp"),
        P(),
        P("tp"),
        P("tp"),
        P("tp"),
        P("tp", None),
    )
    return jax.shard_map(
        body, mesh=mesh, in_specs=placed, out_specs=P(("ctx", "tp"), None), check_vma=False
    )
```

time: 642 us -> 206 us (0.32); the launches traced: 632 us -> 206 us
  waiting for transfers between devices: 355 us -> 0 us
  Pallas kernels: 0 us -> 202 us
  matrix products: 116 us -> 0 us
  blocking collectives: 87.7 us -> 0 us
  other arithmetic: 35.9 us -> 0 us
  between operations: 14.6 us -> 0.03 us
  local copies, waits for them, and re-layouts: 16.9 us -> 3.73 us
    pallas_call x0 -> x3, Pallas kernels: none -> 202 us  [the longest x1 85.5 us: gathered(): pl.pallas_call(gather_kernel, out_shape=(jax.ShapeDtypeStruct((total, wid...]
    all_gather x4 -> x0, waiting for transfers between devices: 176 us -> none  [the longest x1 98.7 us: body(): lax.all_gather(normed_rows, 'tp', axis=0, tiled=True)]
    reduce_scatter x1 -> x0, waiting for transfers between devices: 176 us -> none  [body(): lax.psum_scatter(summed_term, 'tp', scatter_dimension=0, tiled=True)]
    dot_general x21 -> x0, matrix products: 116 us -> none  [the longest x3 26.1 us: within_shard(): local_part = jnp.einsum('hts,shp->thp', weights, inner_act, precision=EXACT)]
    psum x1 -> x0, blocking collectives: 71.5 us -> none  [body(): lax.psum((jnp.sum(gated_out * gated_out, axis=1), jnp.sum(norm_gain * out...]
    unnamed x1 -> x0, blocking collectives: 16.2 us -> none
    select_n x16 -> x0, other arithmetic: 15.9 us -> none  [turn(): return jax.tree.map(lambda a, b: jnp.where(reached, a, b), new, before)]
  transfers between devices with their start and end apart: 7 -> 0, of which waited for: 6 -> 0; matrix products, arithmetic and copies ran while one was open for 11% -> 0% of each run, Pallas kernels for 0% -> 0%
where the time goes in v1:
time: 206 us
  Pallas kernels  202 us (98%)
  local copies, waits for them, and re-layouts  3.73 us (2%)
    pallas_call x1, Pallas kernels, gathered(): pl.pallas_call(gather_kernel, out_shape=(jax.ShapeDtypeStruct((total, wid...  85.5 us
    pallas_call x1, Pallas kernels, mixed(): pl.pallas_call(mixer_kernel, out_shape=(jax.ShapeDtypeStruct((total, widt...  63.3 us
    pallas_call x1, Pallas kernels, scattered(): pl.pallas_call(scatter_kernel, out_shape=jax.ShapeDtypeStruct((rows, dept...  53 us

profile of v1, /device:TPU:1, one launch (start us, length us, event | category | flops | bytes accessed | tf_op | source)
XLA Modules:
  0.0 205.5 jit_solution(1924734777412336420)
XLA Ops:
  0.0 2.1 %copy.12.step_ref = bf16[4096,2]{1,0:T(8,128)(2,1)} copy(bf16[4096,2]{0,1:T(2,128)(2,1)} %param.15) | data formatting | bytes 32768 | tf_op args[4]
  2.1 85.5 %gather_project.1 = (bf16[768,256]{1,0:T(8,128)(2,1)}, bf16[768,512]{1,0:T(8,128)(2,1)}, f32[768,128]{1,0:T(8,128)}, f32[768,256]{1,0:T(8,128)}) custom-call(bf16[24,4096]{1,0:T(8,128)(2,1)} %rows_ref.1, bf16[24,4096]{1,0:T(8,128)(2,1)} %grads_ref.1, bf16[2,4096,256]{2,1,0:T(8,128)(2,1)} %inner_hbm.3, bf16[4096,256]{1,0:T(8,128)(2,1)} %state_hbm.3, ...), custom_call_target="tpu_custom_call" | custom-call | tf_op jit(solution)/shard_map/gather_project/pallas_call | solution.py:244
  87.7 63.3 %mixer.1 = (bf16[768,256]{1,0:T(8,128)(2,1)}, bf16[768,256]{1,0:T(8,128)(2,1)}, bf16[768,256]{1,0:T(8,128)(2,1)}, bf16[768,2]{1,0:T(8,128)(2,1)}) custom-call(f32[2]{0:T(128)} %step_bias_ref.1, f32[2]{0:T(128)} %decay_log_ref.1, bf16[768,256]{1,0:T(8,128)(2,1)} %get-tuple-element.13.gate_ref, bf16[768,512]{1,0:T(8,128)(2,1)} %get-tuple-element.14.conv_ref, ...), custom_call_target="tpu_custom_call" | custom-call | tf_op jit(solution)/shard_map/mixer/pallas_call | solution.py:871
  151.0 53.0 %product_scatter.1 = bf16[24,4096]{1,0:T(8,128)(2,1)} custom-call(bf16[768,256]{1,0:T(8,128)(2,1)} %get-tuple-element.17.gate_ref, bf16[768,256]{1,0:T(8,128)(2,1)} %get-tuple-element.18.inner_ref, bf16[768,256]{1,0:T(8,128)(2,1)} %get-tuple-element.19.dstate_ref, bf16[768,2]{1,0:T(8,128)(2,1)} %get-tuple-element.20.dstep_ref, ...), custom_call_target="tpu_custom_call" | custom-call | tf_op jit(solution)/shard_map/product_scatter/pallas_call | solution.py:478
  203.9 1.6 copy.15

commit v2 on v0

v2 whole, which is shorter than its diff:
```python
import functools
from types import SimpleNamespace

import jax
import jax.numpy as jnp
from jax import lax
from jax.experimental import pallas as pl
from jax.experimental.pallas import tpu as pltpu
from jax.sharding import PartitionSpec as P

HEAD_DIM = 128
STATE = 128
CONV = 4
EPSILON = 1e-05
EXACT = lax.Precision.HIGHEST
MESH = pl.DeviceIdType.MESH
F32 = jnp.float32
BF16 = jnp.bfloat16
VMEM_LIMIT = 62 * 1024 * 1024

Z = 8
GROUP = 4 * Z
ROW = 4
SHARDS = 2 * ROW
CHUNK = 128
HALO = 8
NN, NT, TN = ((1,), (0,)), ((1,), (1,)), ((0,), (0,))


def place():
    tp = lax.axis_index("tp")
    return tp // (2 * Z), lax.rem(tp // 2, Z), lax.rem(tp, 2)


def tp_id(yh, z, core):
    return (yh * Z + lax.rem(z + Z, Z)) * 2 + core


def remote(axis, partner, src, dst, send_sem, recv_sem):
    return pltpu.make_async_remote_copy(
        src_ref=src,
        dst_ref=dst,
        send_sem=send_sem,
        recv_sem=recv_sem,
        device_id={axis: partner},
        device_id_type=MESH,
    )


def dot(a, b, contract, precision=EXACT):
    return lax.dot_general(a, b, (contract, ((), ())), precision=precision, preferred_element_type=F32)


def dot16(a, b, contract):
    return lax.dot_general(a, b, (contract, ((), ())), preferred_element_type=F32)


class Gather:
    def __init__(self, own_ref, buf, swap, send_sem, recv_sem):
        self.own_ref, self.buf, self.swap = own_ref, buf, swap
        self.send_sem, self.recv_sem = send_sem, recv_sem
        self.yh, self.z, self.core = place()
        self.pair = 2 * own_ref.shape[0]
        self.half = own_ref.shape[1] // 2
        self.sibling = tp_id(self.yh, self.z, 1 - self.core)
        self.started = []

    def block(self, h, dz, sub, core=None):
        yh = self.yh if h == 0 else 1 - self.yh
        chip = yh * Z + lax.rem(self.z + (dz + Z), Z)
        rows = pl.ds(pl.multiple_of(chip * self.pair, 16), self.pair)
        quarter = self.half // 2
        at = (self.core if core is None else core) * self.half + sub * quarter
        return self.buf.at[rows, pl.ds(pl.multiple_of(at, quarter), quarter)]

    def copy(self, slot, src, dst, partner):
        return remote("tp", partner, src, dst, self.send_sem.at[slot], self.recv_sem.at[slot])

    def send(self, slot, src, dst, partner):
        copy = self.copy(slot, src, dst, partner)
        copy.start()
        self.started.append(copy)

    def got(self, slot, block):
        self.copy(slot, block, block, self.sibling).wait_recv()

    def across(self, sub, d):
        here = self.block(0, (1 - 2 * sub) * d, sub)
        self.send(sub * 31 + d, here, here, tp_id(1 - self.yh, self.z, self.core))

    def along(self, kind, sub, d):
        way = 1 - 2 * sub
        if kind == "long":
            here = self.block(0, way * (d - 1), sub)
            self.send(sub * 31 + 4 + d, here, here, tp_id(self.yh, self.z - way, self.core))
        elif kind == "short":
            here = self.block(0, -way * (d - 1), sub)
            self.send(sub * 31 + 9 + d, here, here, tp_id(self.yh, self.z + way, self.core))
        else:
            here = self.block(1, -way * (d - 1), sub)
            self.send(sub * 31 + 11 + d, here, here, tp_id(self.yh, self.z + way, self.core))

    def sibling_slot(self, h, dz, sub):
        return sub * 31 + 15 + h * 8 + dz % 8

    def to_sibling(self, h, dz, sub):
        here = self.block(h, dz, sub)
        self.send(self.sibling_slot(h, dz, sub), here, here, self.sibling)

    def first_swap(self):
        columns = pl.ds(pl.multiple_of((1 - self.core) * self.half, self.half), self.half)
        self.send(62, self.own_ref.at[:, columns], self.swap, self.sibling)

    def begin(self):
        self.got(62, self.swap)
        columns = pl.ds(pl.multiple_of(self.core * self.half, self.half), self.half)
        mine = self.own_ref[:, columns].astype(F32)
        other = self.swap[...].astype(F32)
        first = self.core == 0
        both = jnp.concatenate([jnp.where(first, mine, other), jnp.where(first, other, mine)], axis=0)
        quarter = self.half // 2
        for sub in (0, 1):
            self.block(0, 0, sub)[...] = both[:, sub * quarter : (sub + 1) * quarter].astype(BF16)
        for sub in (0, 1):
            self.along("long", sub, 1)
            self.across(sub, 0)
            self.along("short", sub, 1)
            self.to_sibling(0, 0, sub)

    def long(self, d):
        for sub in (0, 1):
            dz = (1 - 2 * sub) * d
            self.got(sub * 31 + 4 + d, self.block(0, dz, sub))
            if d < 5:
                self.along("long", sub, d + 1)
                self.across(sub, d)
            self.to_sibling(0, dz, sub)

    def short(self, d):
        for sub in (0, 1):
            dz = -(1 - 2 * sub) * d
            self.got(sub * 31 + 9 + d, self.block(0, dz, sub))
            if d < 2:
                self.along("short", sub, d + 1)
            self.to_sibling(0, dz, sub)

    def met(self, d):
        for sub in (0, 1):
            dz = (1 - 2 * sub) * d
            self.got(sub * 31 + d, self.block(1, dz, sub))
            if d == 0:
                self.along("other", sub, 1)
            self.to_sibling(1, dz, sub)

    def other(self, d):
        for sub in (0, 1):
            dz = -(1 - 2 * sub) * d
            self.got(sub * 31 + 11 + d, self.block(1, dz, sub))
            if d < 3:
                self.along("other", sub, d + 1)
            self.to_sibling(1, dz, sub)

    def steps(self):
        order = [
            (self.long, 1), (self.short, 1), (self.met, 0), (self.long, 2), (self.short, 2), (self.met, 1),
            (self.other, 1), (self.long, 3), (self.met, 2), (self.other, 2), (self.long, 4), (self.met, 3),
            (self.other, 3), (self.long, 5), (self.met, 4),
        ]
        return [functools.partial(step, d) for step, d in order]

    def finish(self):
        for sub in (0, 1):
            for h in (0, 1):
                for dz in range(8):
                    self.got(self.sibling_slot(h, dz, sub), self.block(h, dz, sub, 1 - self.core))

    def drain(self):
        for copy in self.started:
            copy.wait_send()


class Scatter:
    order = (-3, 3, -4, 2, -2, 1, -1, 0)

    def __init__(self, r, rows, depth):
        self.r = r
        self.yh, self.z, self.core = place()
        self.sibling = tp_id(self.yh, self.z, 1 - self.core)
        self.rows, self.pair, self.half = rows, 2 * rows, depth // 2
        self.quarter = self.half // 2
        self.tile = 512
        self.started = []

    def at(self, dz):
        return self.order.index(dz if dz < 4 and dz > -4 else -4 if abs(dz) == 4 else dz - 8 if dz > 0 else dz + 8)

    def start(self, copy):
        copy.start()
        self.started.append(copy)

    def product(self, dz):
        r, at, half, tile = self.r, self.at(dz), self.half, self.tile
        zt = lax.rem(self.z + (dz + Z), Z)
        spots = []
        for h in (0, 1):
            yt = self.yh if h == 0 else 1 - self.yh
            spots.append(pl.ds(pl.multiple_of((yt * Z + zt) * self.pair, 16), self.pair))

        def side(which, keep):
            def turn(j, carry):
                here = pl.ds(pl.multiple_of(j * tile, tile), tile)
                cols = pl.ds(pl.multiple_of(which * half + j * tile, tile), tile)
                parts = []
                for ref in (r.d_gate, r.d_inner, r.d_state, r.d_step):
                    parts.append(jnp.concatenate([ref[spots[0], :], ref[spots[1], :]], axis=0))
                value = dot16(parts[0], r.inner_w[0, cols, :], NT)
                value += dot16(parts[1], r.inner_w[1, cols, :], NT)
                value += dot16(parts[2], r.state_w[cols, :], NT)
                value += dot16(parts[3], r.step_w[:, cols], NN)
                for h in (0, 1):
                    keep[at, h, :, here] = value[h * self.pair : (h + 1) * self.pair].astype(keep.dtype)
                return carry

            lax.fori_loop(0, half // tile, turn, 0)

        side(1 - self.core, r.sib_out)
        self.start(
            remote("tp", self.sibling, r.sib_out.at[at], r.sib_in.at[at], r.sib_send.at[at], r.sib_recv.at[at])
        )
        side(self.core, r.mine)

    def sib_got(self, dz):
        at, r = self.at(dz), self.r
        there = r.sib_in.at[at]
        remote("tp", self.sibling, there, there, r.sib_send.at[at], r.sib_recv.at[at]).wait_recv()

    def got(self, slot):
        there = self.r.ring_in.at[slot]
        remote("tp", self.sibling, there, there, self.r.ring_send.at[slot], self.r.ring_recv.at[slot]).wait_recv()

    def slot(self, kind, sub, d):
        return sub * 15 + {"y": 0, "long": 4, "short": 9, "other": 11}[kind] + d

    def value(self, h, dz, sub, slots, columns):
        at, r = self.at(dz), self.r
        here = pl.ds(pl.multiple_of(sub * self.quarter + columns, self.tile), self.tile)
        there = pl.ds(pl.multiple_of(columns, self.tile), self.tile)
        total = r.mine[at, h, :, here] + r.sib_in[at, h, :, here].astype(F32)
        for slot in slots:
            total += r.ring_in[slot, :, there].astype(F32)
        return total

    def message(self, kind, sub, d):
        way = 1 - 2 * sub
        earlier = []
        if kind == "y":
            h, dz, partner = 1, way * d, tp_id(1 - self.yh, self.z, self.core)
            if d == 0:
                earlier.append(self.slot("other", sub, 1))
        elif kind == "long":
            h, dz, partner = 0, way * d, tp_id(self.yh, self.z + way, self.core)
            if d < 5:
                earlier += [self.slot("long", sub, d + 1), self.slot("y", sub, d)]
        elif kind == "short":
            h, dz, partner = 0, -way * d, tp_id(self.yh, self.z - way, self.core)
            if d < 2:
                earlier.append(self.slot("short", sub, d + 1))
        else:
            h, dz, partner = 1, -way * d, tp_id(self.yh, self.z - way, self.core)
            if d < 3:
                earlier.append(self.slot("other", sub, d + 1))
        for slot in earlier:
            self.got(slot)
        slot, r = self.slot(kind, sub, d), self.r

        def turn(j, carry):
            columns = j * self.tile
            there = pl.ds(pl.multiple_of(columns, self.tile), self.tile)
            r.ring_out[slot, :, there] = self.value(h, dz, sub, earlier, columns).astype(BF16)
            return carry

        lax.fori_loop(0, self.quarter // self.tile, turn, 0)
        self.start(
            remote("tp", partner, r.ring_out.at[slot], r.ring_in.at[slot], r.ring_send.at[slot], r.ring_recv.at[slot])
        )

    def run(self, out_ref):
        r, core, half = self.r, self.core, self.half

        def both(kind, d):
            for sub in (0, 1):
                self.message(kind, sub, d)

        self.product(-3)
        self.product(3)
        self.sib_got(-3)
        self.message("long", 0, 5)
        self.message("other", 0, 3)
        self.message("y", 1, 3)
        self.product(-4)
        self.sib_got(3)
        self.message("long", 1, 5)
        self.message("other", 1, 3)
        self.message("y", 0, 3)
        self.product(2)
        self.sib_got(-4)
        both("y", 4)
        self.product(-2)
        both("long", 4)
        self.sib_got(2)
        self.message("short", 1, 2)
        self.message("y", 0, 2)
        self.sib_got(-2)
        self.message("short", 0, 2)
        self.message("y", 1, 2)
        self.product(1)
        both("other", 2)
        both("long", 3)
        self.product(-1)
        self.sib_got(1)
        self.sib_got(-1)
        both("y", 1)
        both("other", 1)
        both("short", 1)
        self.product(0)
        both("long", 2)
        self.sib_got(0)
        both("y", 0)
        both("long", 1)
        first = core == 0
        for sub in (0, 1):
            earlier = [self.slot(*key) for key in (("short", sub, 1), ("y", sub, 0), ("long", sub, 1))]
            for slot in earlier:
                self.got(slot)

            def final(j, carry, sub=sub, earlier=earlier):
                columns = j * self.tile
                value = self.value(0, 0, sub, earlier, columns)
                low, high = value[: self.rows], value[self.rows :]
                at = sub * self.quarter + columns
                here = pl.ds(pl.multiple_of(core * half + at, self.tile), self.tile)
                out_ref[:, here] = jnp.where(first, low, high).astype(BF16)
                there = pl.ds(pl.multiple_of(columns, self.tile), self.tile)
                r.last_out[sub, :, there] = jnp.where(first, high, low).astype(BF16)
                return carry

            lax.fori_loop(0, self.quarter // self.tile, final, 0)
            self.start(
                remote(
                    "tp", self.sibling, r.last_out.at[sub], r.last_in.at[sub], r.last_send.at[sub], r.last_recv.at[sub]
                )
            )
        for sub in (0, 1):
            there = r.last_in.at[sub]
            remote("tp", self.sibling, there, there, r.last_send.at[sub], r.last_recv.at[sub]).wait_recv()
            at = (1 - core) * half + sub * self.quarter
            out_ref[:, pl.ds(pl.multiple_of(at, self.quarter), self.quarter)] = r.last_in[sub]
        for copy in self.started:
            copy.wait_send()


class Exchange:
    def __init__(self, out, into, cross_out, cross_in, send_sem, recv_sem, factors_in, heads, forward):
        self.ctx = lax.axis_index("ctx")
        self.x, self.y = lax.rem(self.ctx, ROW), self.ctx // ROW
        self.out, self.into, self.heads, self.forward = out, into, heads, forward
        self.factors_in, self.cross_out, self.cross_in = factors_in, cross_out, cross_in
        self.gives = self.y == (0 if forward else 1)
        self.copies = [
            remote("ctx", self.peer(j), out, into.at[j - 1], send_sem.at[j - 1], recv_sem.at[j - 1])
            for j in range(1, ROW)
        ]
        self.cross = remote(
            "ctx", lax.rem(self.ctx + ROW, SHARDS), cross_out, cross_in, send_sem.at[ROW - 1], recv_sem.at[ROW - 1]
        )

    def peer(self, j):
        return self.y * ROW + lax.rem(self.x + j, ROW)

    def start(self):
        for copy in self.copies:
            copy.start()

    def step(self, value, slot):
        parts = []
        for h in range(self.heads):
            state = self.into[slot, h * HEAD_DIM : (h + 1) * HEAD_DIM, :].astype(F32)
            parts.append(value[h] * self.factors_in[slot, h : h + 1, :] + state)
        return parts

    def chain(self, total):
        for j in range(ROW - 1, 0, -1):
            there = self.x >= j if self.forward else self.x + j < ROW
            slot = j - 1 if self.forward else ROW - 1 - j

            @pl.when(there)
            def _(slot=slot):
                for h, part in enumerate(self.step([total[h] for h in range(self.heads)], slot)):
                    total[h] = part

    def give(self, total, own, factors):
        for copy in self.copies:
            copy.wait_recv()

        @pl.when(self.gives)
        def _():
            total[...] = jnp.zeros_like(total)
            self.chain(total)
            for h in range(self.heads):
                self.cross_sum[h] = total[h] * factors[h : h + 1, :] + own[h]
            for j in range(1, ROW):
                there = self.x + j < ROW if self.forward else self.x >= j
                slot = ROW - 1 - j if self.forward else j - 1

                @pl.when(there)
                def _(slot=slot):
                    for h, part in enumerate(self.step([self.cross_sum[h] for h in range(self.heads)], slot)):
                        self.cross_sum[h] = part

            for h in range(self.heads):
                self.cross_out[h * HEAD_DIM : (h + 1) * HEAD_DIM, :] = self.cross_sum[h]
            self.cross.start()

    def take(self, total):
        @pl.when(jnp.logical_not(self.gives))
        def _():
            self.cross.wait_recv()
            for h in range(self.heads):
                total[h] = self.cross_in[h * HEAD_DIM : (h + 1) * HEAD_DIM, :].astype(F32)
            self.chain(total)

    def drain(self):
        for copy in self.copies:
            copy.wait_send()

        @pl.when(self.gives)
        def _():
            self.cross.wait_send()


def mixer_forward(r, tick):
    ctx = lax.axis_index("ctx")
    total, both = r.conv.shape
    width = both - 2 * STATE
    heads = width // HEAD_DIM
    chunks = total // CHUNK
    span = lambda k: slice(k * CHUNK, (k + 1) * CHUNK)
    r.ext[HALO:, :] = r.conv[...].astype(F32)
    halo = remote("ctx", lax.rem(ctx + 1, SHARDS), r.ext.at[total:, :], r.ext.at[:HALO, :], r.halo_sem.at[0], r.halo_sem.at[1])

    @pl.when(ctx < SHARDS - 1)
    def _():
        halo.start()

    lane = lax.broadcasted_iota(jnp.int32, (1, CHUNK), 1)
    rows_at = lax.broadcasted_iota(jnp.int32, (CHUNK, CHUNK), 0)
    cols_at = lax.broadcasted_iota(jnp.int32, (CHUNK, CHUNK), 1)
    causal = (rows_at >= cols_at).astype(F32)

    def per_lane(values):
        row = jnp.zeros_like(values[0])
        for h, value in enumerate(values):
            row = jnp.where(lane == h, value, row)
        return row

    bias = per_lane([jnp.full((1, CHUNK), r.step_bias[h], F32) for h in range(heads)])
    rate = per_lane([jnp.exp(jnp.full((1, CHUNK), r.decay_log[h], F32)) for h in range(heads)])
    valid = lane < heads
    kernel = [
        jnp.concatenate([r.conv_inner[k : k + 1, :], r.conv_state[k : k + 1, :]], axis=1) for k in range(CONV)
    ]
    ends = []
    for k in range(chunks):
        raw = jnp.where(valid, r.stepraw[span(k), :], 0.0) + bias
        step = jnp.maximum(raw, 0.0) + jnp.log1p(jnp.exp(-jnp.abs(raw)))
        step = jnp.where(valid, step, 0.0)
        r.steps[span(k), :] = step
        cum = dot(causal, -step * rate, NN)
        r.cums[span(k), :] = cum
        turned = cum.T
        ends.append([cum[CHUNK - 1 :, h : h + 1] for h in range(heads)])
        for h in range(heads):
            spread = cum[:, h : h + 1] - turned[h : h + 1, :]
            r.decays[k, h] = jnp.exp(jnp.minimum(spread, 0.0)) * causal
    tick()

    @pl.when(ctx == 0)
    def _():
        r.ext[:HALO, :] = jnp.zeros((HALO, both), F32)

    @pl.when(ctx > 0)
    def _():
        halo.wait_recv()

    for k in range(chunks):
        blended = jnp.zeros((CHUNK, both), F32)
        for tap in range(CONV):
            start = k * CHUNK + HALO - (CONV - 1) + tap
            blended += kernel[tap] * r.ext[start : start + CHUNK, :]
        r.pre[span(k), :] = blended
        active = blended * jax.nn.sigmoid(blended)
        r.act[span(k), :] = active
        b_rows, c_rows = active[:, width : width + STATE], active[:, width + STATE :]
        r.cb[k] = dot(c_rows, b_rows, NT)
        for h in range(heads):
            lanes = slice(h * HEAD_DIM, (h + 1) * HEAD_DIM)
            fed = active[:, lanes] * r.steps[span(k), h : h + 1]
            r.xd[span(k), lanes] = fed
            left = jnp.exp(ends[k][h] - r.cums[span(k), h : h + 1])
            own = dot(fed * left, b_rows, TN)
            if k == 0:
                r.states[0, h] = jnp.zeros_like(own)
                r.states[1, h] = own
            else:
                r.states[k + 1, h] = jnp.exp(ends[k][h]) * r.states[k, h] + own
        if k % 3 == 2:
            tick()

    befores = [[jnp.zeros((1, 1), F32) for _ in range(heads)]]
    for k in range(chunks):
        befores.append([befores[k][h] + ends[k][h] for h in range(heads)])
    whole = [jnp.exp(befores[chunks][h]) for h in range(heads)]
    row8 = lax.broadcasted_iota(jnp.int32, (8, CHUNK), 0)
    factors = jnp.zeros((8, CHUNK), F32)
    for h in range(heads):
        r.fwd_out[h * HEAD_DIM : (h + 1) * HEAD_DIM, :] = r.states[chunks, h]
        factors = jnp.where(row8 == h, whole[h], factors)
    r.factors_out[...] = factors
    forward = Exchange(
        r.fwd_out, r.fwd_in, r.cross_out.at[0], r.cross_in.at[0], r.fwd_send, r.fwd_recv, r.factors_in, heads, True
    )
    forward.cross_sum = r.cross_sum
    factor_copies = [
        remote(
            "ctx", forward.peer(j), r.factors_out, r.factors_in.at[j - 1], r.factor_send.at[j - 1], r.factor_recv.at[j - 1]
        )
        for j in range(1, ROW)
    ]
    for copy in factor_copies:
        copy.start()
    forward.start()
    tick()

    for k in range(chunks):
        c_rows = r.act[span(k), width + STATE :]
        for h in range(heads):
            lanes = slice(h * HEAD_DIM, (h + 1) * HEAD_DIM)
            value = dot(r.decays[k, h] * r.cb[k], r.xd[span(k), lanes], NN)
            if k > 0:
                value += jnp.exp(r.cums[span(k), h : h + 1]) * dot(c_rows, r.states[k, h], NT)
            r.out[span(k), lanes] = value
        if k % 3 == 2:
            tick()

    for copy in factor_copies:
        copy.wait_recv()
    forward.give(r.entering, r.states.at[chunks], factors)
    tick()
    forward.take(r.entering)
    tick()
    for k in range(chunks):
        c_rows = r.act[span(k), width + STATE :]
        for h in range(heads):
            lanes = slice(h * HEAD_DIM, (h + 1) * HEAD_DIM)
            grown = jnp.exp(r.cums[span(k), h : h + 1] + befores[k][h])
            r.out[span(k), lanes] = r.out[span(k), lanes] + grown * dot(c_rows, r.entering[h], NT)
            r.states[k, h] = r.states[k, h] + jnp.exp(befores[k][h]) * r.entering[h]
        if k % 2 == 1:
            tick()
    for h in range(heads):
        r.states[chunks, h] = r.states[chunks, h] + whole[h] * r.entering[h]

    def drain():
        @pl.when(ctx < SHARDS - 1)
        def _():
            halo.wait_send()

        for copy in factor_copies:
            copy.wait_send()
        forward.drain()

    return SimpleNamespace(
        total=total, both=both, width=width, heads=heads, chunks=chunks, span=span, lane=lane, bias=bias, rate=rate,
        valid=valid, kernel=kernel, ends=ends, factors=factors, drain=drain, rows_at=rows_at, cols_at=cols_at,
    )


def token_sums(r, f):
    gain = r.gain[...]
    ones = jnp.ones((8, f.width), F32)
    for k in range(f.chunks):
        gate = r.gate[f.span(k), :].astype(F32)
        gated = r.out[f.span(k), :] * (gate * jax.nn.sigmoid(gate))
        squares = dot(ones, gated * gated, NT)
        crosses = dot(ones, gain * r.local[f.span(k), :] * gated, NT)
        r.tot_out[0, 0:1, f.span(k)] = squares[0:1, :]
        r.tot_out[0, 1:2, f.span(k)] = crosses[0:1, :]
    yh, z, core = place()
    copies = []

    def swap(phase, partners, base):
        mine = []
        for j, partner in enumerate(partners):
            slot = base + j
            copy = remote(
                "tp", partner, r.tot_out.at[phase], r.tot_in.at[slot], r.tot_send.at[slot], r.tot_recv.at[slot]
            )
            copy.start()
            mine.append(copy)
        sums = r.tot_out[phase]
        for j, copy in enumerate(mine):
            copy.wait_recv()
            sums = sums + r.tot_in[base + j]
        copies.extend(mine)
        return sums

    near = [tp_id(yh, z, 1 - core), tp_id(1 - yh, z, core), tp_id(1 - yh, z, 1 - core)]
    r.tot_out[1] = swap(0, near, 0)
    sums = swap(1, [tp_id(yh, z + j, core) for j in range(1, Z)], len(near))
    return sums, copies


def mixer_backward(r, f, sums):
    ctx = lax.axis_index("ctx")
    span, chunks, heads, width, total = f.span, f.chunks, f.heads, f.width, f.total
    channels = width * GROUP
    gain = r.gain[...]
    anti = (f.rows_at <= f.cols_at).astype(F32)
    ends = f.ends
    for k in range(chunks):
        held = jnp.concatenate([sums[:, span(k)], jnp.zeros((CHUNK - 2, CHUNK), F32)], axis=0).T
        inverse = lax.rsqrt(held[:, 0:1] / channels + EPSILON)
        pull = inverse * inverse * inverse * (held[:, 1:2] / channels)
        gate = r.gate[span(k), :].astype(F32)
        sigmoid = jax.nn.sigmoid(gate)
        opened = gate * sigmoid
        value = r.out[span(k), :]
        d_gated = inverse * (gain * r.local[span(k), :]) - value * opened * pull
        r.d_gate[span(k), :] = (d_gated * value * sigmoid * (1.0 + gate * (1.0 - sigmoid))).astype(BF16)
        r.dy[span(k), :] = d_gated * opened

    for k in range(chunks - 1, -1, -1):
        c_rows = r.act[span(k), width + STATE :]
        for h in range(heads):
            lanes = slice(h * HEAD_DIM, (h + 1) * HEAD_DIM)
            own = dot(r.dy[span(k), lanes] * jnp.exp(r.cums[span(k), h : h + 1]), c_rows, TN)
            if k < chunks - 1:
                own += jnp.exp(ends[k][h]) * r.d_states[k + 1, h]
            r.d_states[k, h] = own
    for h in range(heads):
        r.bwd_out[h * HEAD_DIM : (h + 1) * HEAD_DIM, :] = r.d_states[0, h]
    backward = Exchange(
        r.bwd_out, r.bwd_in, r.cross_out.at[1], r.cross_in.at[1], r.bwd_send, r.bwd_recv, r.factors_in, heads, False
    )
    backward.cross_sum = r.cross_sum
    backward.start()

    def local(k):
        b_rows, c_rows = r.act[span(k), width : width + STATE], r.act[span(k), width + STATE :]
        d_cb = jnp.zeros((CHUNK, CHUNK), F32)
        d_crows = jnp.zeros((CHUNK, STATE), F32)
        for h in range(heads):
            lanes = slice(h * HEAD_DIM, (h + 1) * HEAD_DIM)
            grad = r.dy[span(k), lanes]
            d_cb += r.decays[k, h] * dot(grad, r.xd[span(k), lanes], NT)
            r.u_loc[span(k), lanes] = dot(r.decays[k, h] * r.cb[k], grad, TN)
            d_crows += jnp.exp(r.cums[span(k), h : h + 1]) * dot(grad, r.states[k, h], NN)
        r.d_b[span(k), :] = dot(d_cb, c_rows, TN)
        r.d_c[span(k), :] = d_crows + dot(d_cb, b_rows, NN)

    for k in range(chunks // 2):
        local(k)
    backward.give(r.d_leaving, r.d_states.at[0], f.factors)
    for k in range(chunks // 2, chunks):
        local(k)
    backward.take(r.d_leaving)
    after = [jnp.zeros((1, 1), F32) for _ in range(heads)]
    for h in range(heads):
        r.d_states[chunks, h] = r.d_leaving[h]
    for k in range(chunks - 1, 0, -1):
        after = [after[h] + ends[k][h] for h in range(heads)]
        for h in range(heads):
            r.d_states[k, h] = r.d_states[k, h] + jnp.exp(after[h]) * r.d_leaving[h]

    halo = remote("ctx", lax.rem(ctx + SHARDS - 1, SHARDS), r.d_pre.at[:HALO, :], r.d_pre.at[total:, :], r.halo_sem.at[2], r.halo_sem.at[3])
    for k in range(chunks):
        b_rows = r.act[span(k), width : width + STATE]
        d_brows = r.d_b[span(k), :]
        d_acts = []
        pulls = jnp.zeros((CHUNK, CHUNK), F32)
        feeds = jnp.zeros((CHUNK, CHUNK), F32)
        edge = jnp.zeros((1, CHUNK), F32)
        for h in range(heads):
            lanes = slice(h * HEAD_DIM, (h + 1) * HEAD_DIM)
            step = r.steps[span(k), h : h + 1]
            left = jnp.exp(ends[k][h] - r.cums[span(k), h : h + 1])
            d_next = r.d_states[k + 1, h]
            grad = r.u_loc[span(k), lanes] + left * dot(b_rows, d_next, NT)
            d_brows += dot(r.xd[span(k), lanes] * left, d_next, NN)
            d_acts.append(grad * step)
            fed = jnp.sum(grad * r.act[span(k), lanes], axis=1, keepdims=True)
            met = jnp.sum(r.dy[span(k), lanes] * r.out[span(k), lanes], axis=1, keepdims=True)
            pulls = jnp.where(f.lane == h, met - step * fed, pulls)
            feeds = jnp.where(f.lane == h, fed, feeds)
            edge = jnp.where(f.lane == h, jnp.sum(d_next * r.states[k + 1, h]), edge)
        d_decay = dot(anti, pulls, NN) + edge
        raw = jnp.where(f.valid, r.stepraw[span(k), :], 0.0) + f.bias
        d_raw = (feeds - f.rate * d_decay) * jax.nn.sigmoid(raw)
        r.d_step[span(k), :] = d_raw[:, :heads].astype(BF16)
        d_act = jnp.concatenate(d_acts + [d_brows, r.d_c[span(k), :]], axis=1)
        value = r.pre[span(k), :]
        sigmoid = jax.nn.sigmoid(value)
        r.d_pre[span(k), :] = d_act * sigmoid * (1.0 + value * (1.0 - sigmoid))
        if k == 0:

            @pl.when(ctx > 0)
            def _():
                halo.start()

    @pl.when(ctx == SHARDS - 1)
    def _():
        r.d_pre[total:, :] = jnp.zeros((HALO, f.both), F32)

    @pl.when(ctx < SHARDS - 1)
    def _():
        halo.wait_recv()

    for k in range(chunks):
        blended = jnp.zeros((CHUNK, f.both), F32)
        for tap in range(CONV):
            start = k * CHUNK + CONV - 1 - tap
            blended += f.kernel[tap] * r.d_pre[start : start + CHUNK, :]
        r.d_inner[span(k), :] = blended[:, :width].astype(BF16)
        r.d_state[span(k), :] = blended[:, width:].astype(BF16)

    def drain():
        @pl.when(ctx > 0)
        def _():
            halo.wait_send()

        backward.drain()

    return drain


def whole_kernel(names, *refs):
    r = SimpleNamespace(**dict(zip(names, refs, strict=True)))
    loads = [
        pltpu.make_async_copy(src, dst, r.weight_sem.at[i])
        for i, (src, dst) in enumerate(
            ((r.inner_hbm, r.inner_w), (r.state_hbm, r.state_w), (r.out_hbm, r.out_w), (r.step_hbm, r.step_w))
        )
    ]
    for load in loads:
        load.start()
    yh, z, core = place()
    ctx = lax.axis_index("ctx")
    barrier = pltpu.get_barrier_semaphore()
    tp_partners = [tp_id(yh, z, 1 - core), tp_id(1 - yh, z, core), tp_id(1 - yh, z, 1 - core)]
    tp_partners += [tp_id(yh, z + j, core) for j in range(1, Z)]
    row = ctx // ROW * ROW
    ctx_partners = [row + lax.rem(ctx - row + j, ROW) for j in range(1, ROW)]
    ctx_partners += [lax.rem(ctx + j, SHARDS) for j in (ROW, 1, SHARDS - 1)]
    for axis, partners in (("tp", tp_partners), ("ctx", ctx_partners)):
        for partner in partners:
            pl.semaphore_signal(barrier, inc=1, device_id={axis: partner}, device_id_type=MESH)
    pl.semaphore_wait(barrier, len(tp_partners) + len(ctx_partners))

    first = Gather(r.rows, r.rows_all, r.swaps.at[0], r.send_r, r.recv_r)
    second = Gather(r.grads, r.grads_all, r.swaps.at[1], r.send_g, r.recv_g)
    first.first_swap()
    second.first_swap()
    first.begin()
    early, late = first.steps()[:-3], first.steps()[-3:]
    for step in early:
        step()
    second.begin()
    pending = second.steps()
    for step in late:
        step()
        pending.pop(0)()
    for load in loads:
        load.wait()
    first.finish()

    def tick():
        if pending:
            pending.pop(0)()

    total, tile = r.rows_all.shape[0], 128

    def project(dst, column, weight, source, contract):
        def tiles(low, high):
            def turn(i, carry):
                at = pl.ds(pl.multiple_of(i * tile, tile), tile)
                value = dot16(source[at, :], weight[...], contract)
                if dst.dtype == F32 and source is r.rows_all:
                    value = value.astype(BF16)
                dst[at, pl.ds(column, value.shape[1])] = value.astype(dst.dtype)
                return carry

            lax.fori_loop(low, high, turn, 0)

        tiles(0, total // tile // 2)
        tick()
        tiles(total // tile // 2, total // tile)
        tick()

    width = r.inner_w.shape[2]
    project(r.conv, 0, r.inner_w.at[1], r.rows_all, NN)
    project(r.conv, width, r.state_w, r.rows_all, NN)
    project(r.stepraw, 0, r.step_w, r.rows_all, NT)
    project(r.gate, 0, r.inner_w.at[0], r.rows_all, NN)
    f = mixer_forward(r, tick)
    while pending:
        tick()
    second.finish()
    project(r.local, 0, r.out_w, r.grads_all, NT)
    sums, total_copies = token_sums(r, f)
    drain = mixer_backward(r, f, sums)
    rows, depth = r.result.shape
    Scatter(r, rows, depth).run(r.result)
    f.drain()
    drain()
    for copy in total_copies:
        copy.wait_send()
    first.drain()
    second.drain()


def body(
    normed_rows,
    out_grad,
    inner_weight,
    state_weight,
    step_weight,
    conv_inner,
    conv_state,
    step_bias,
    decay_log,
    norm_gain,
    out_weight,
):
    count, depth = normed_rows.shape
    total = count * GROUP
    width, state_width = inner_weight.shape[2], state_weight.shape[1]
    both = width + state_width
    heads = width // HEAD_DIM
    chunks = total // CHUNK
    pair, half = 2 * count, depth // 2
    quarter = half // 2
    vmem = pl.BlockSpec(memory_space=pltpu.VMEM)
    smem = pl.BlockSpec(memory_space=pltpu.SMEM)
    anywhere = pl.BlockSpec(memory_space=pl.ANY)
    inputs = {
        "step_bias": (step_bias, smem),
        "decay_log": (decay_log, smem),
        "rows": (normed_rows, vmem),
        "grads": (out_grad, vmem),
        "conv_inner": (conv_inner, vmem),
        "conv_state": (conv_state, vmem),
        "gain": (norm_gain.reshape(1, -1), vmem),
        "inner_hbm": (inner_weight, anywhere),
        "state_hbm": (state_weight, anywhere),
        "out_hbm": (out_weight, anywhere),
        "step_hbm": (step_weight.T, anywhere),
    }
    state = (heads, HEAD_DIM, STATE)
    message = (heads * HEAD_DIM, STATE)
    scratch = {
        "rows_all": ((total, depth), BF16),
        "grads_all": ((total, depth), BF16),
        "swaps": ((2, count, half), BF16),
        "inner_w": (inner_weight.shape, BF16),
        "state_w": (state_weight.shape, BF16),
        "out_w": (out_weight.shape, BF16),
        "step_w": (step_weight.shape[::-1], BF16),
        "gate": ((total, width), BF16),
        "conv": ((total, both), BF16),
        "stepraw": ((total, CHUNK), F32),
        "local": ((total, width), F32),
        "ext": ((HALO + total, both), F32),
        "pre": ((total, both), F32),
        "act": ((total, both), F32),
        "xd": ((total, width), F32),
        "steps": ((total, CHUNK), F32),
        "cums": ((total, CHUNK), F32),
        "cb": ((chunks, CHUNK, CHUNK), F32),
        "decays": ((chunks, heads, CHUNK, CHUNK), F32),
        "out": ((total, width), F32),
        "dy": ((total, width), F32),
        "states": ((chunks + 1,) + state, F32),
        "d_states": ((chunks + 1,) + state, F32),
        "entering": (state, F32),
        "d_leaving": (state, F32),
        "fwd_out": (message, F32),
        "fwd_in": ((ROW - 1,) + message, F32),
        "bwd_out": (message, F32),
        "bwd_in": ((ROW - 1,) + message, F32),
        "cross_out": ((2,) + message, F32),
        "cross_in": ((2,) + message, F32),
        "cross_sum": (state, F32),
        "factors_out": ((8, CHUNK), F32),
        "factors_in": ((ROW - 1, 8, CHUNK), F32),
        "tot_out": ((2, 2, total), F32),
        "tot_in": ((3 + Z - 1, 2, total), F32),
        "d_pre": ((total + HALO, both), F32),
        "d_b": ((total, STATE), F32),
        "d_c": ((total, STATE), F32),
        "u_loc": ((total, width), F32),
        "d_gate": ((total, width), BF16),
        "d_inner": ((total, width), BF16),
        "d_state": ((total, state_width), BF16),
        "d_step": ((total, heads), BF16),
        "mine": ((Z, 2, pair, half), F32),
        "sib_out": ((Z, 2, pair, half), BF16),
        "sib_in": ((Z, 2, pair, half), BF16),
        "ring_out": ((30, pair, quarter), BF16),
        "ring_in": ((30, pair, quarter), BF16),
        "last_out": ((2, count, quarter), BF16),
        "last_in": ((2, count, quarter), BF16),
    }
    semaphores = {
        "weight_sem": 4,
        "send_r": 63,
        "recv_r": 63,
        "send_g": 63,
        "recv_g": 63,
        "halo_sem": 4,
        "factor_send": ROW - 1,
        "factor_recv": ROW - 1,
        "fwd_send": ROW,
        "fwd_recv": ROW,
        "bwd_send": ROW,
        "bwd_recv": ROW,
        "tot_send": 3 + Z - 1,
        "tot_recv": 3 + Z - 1,
        "sib_send": Z,
        "sib_recv": Z,
        "ring_send": 30,
        "ring_recv": 30,
        "last_send": 2,
        "last_recv": 2,
    }
    names = list(inputs) + ["result"] + list(scratch) + list(semaphores)
    return pl.pallas_call(
        functools.partial(whole_kernel, names),
        out_shape=jax.ShapeDtypeStruct((count, depth), BF16),
        in_specs=[spec for _, spec in inputs.values()],
        out_specs=vmem,
        scratch_shapes=[pltpu.VMEM(shape, dtype) for shape, dtype in scratch.values()]
        + [pltpu.SemaphoreType.DMA((n,)) for n in semaphores.values()],
        compiler_params=pltpu.CompilerParams(collective_id=0, has_side_effects=True, vmem_limit_bytes=VMEM_LIMIT),
        name="mixer_grad",
    )(*[value for value, _ in inputs.values()])


def solution(mesh):
    placed = (
        P(("ctx", "tp"), None),
        P(("ctx", "tp"), None),
        P(None, None, "tp"),
        P(),
        P(None, "tp"),
        P(None, "tp"),
        P(),
        P("tp"),
        P("tp"),
        P("tp"),
        P("tp", None),
    )
    return jax.shard_map(
        body, mesh=mesh, in_specs=placed, out_specs=P(("ctx", "tp"), None), check_vma=False
    )
```

time: 642 us -> 158 us (0.25); the launches traced: 632 us -> 158 us
  waiting for transfers between devices: 355 us -> 0 us
  Pallas kernels: 0 us -> 157 us
  matrix products: 116 us -> 0 us
  blocking collectives: 87.7 us -> 0 us
  other arithmetic: 35.9 us -> 0 us
  local copies, waits for them, and re-layouts: 16.9 us -> 1.62 us
  between operations: 14.6 us -> 0.01 us
    all_gather x4 -> x0, waiting for transfers between devices: 176 us -> none  [the longest x1 98.7 us: body(): lax.all_gather(normed_rows, 'tp', axis=0, tiled=True)]
    reduce_scatter x1 -> x0, waiting for transfers between devices: 176 us -> none  [body(): lax.psum_scatter(summed_term, 'tp', scatter_dimension=0, tiled=True)]
    pallas_call x0 -> x1, Pallas kernels: none -> 157 us  [body(): pl.pallas_call(functools.partial(whole_kernel, names), out_shape=jax.Shap...]
    dot_general x21 -> x0, matrix products: 116 us -> none  [the longest x3 26.1 us: within_shard(): local_part = jnp.einsum('hts,shp->thp', weights, inner_act, precision=EXACT)]
    psum x1 -> x0, blocking collectives: 71.5 us -> none  [body(): lax.psum((jnp.sum(gated_out * gated_out, axis=1), jnp.sum(norm_gain * out...]
    unnamed x1 -> x0, blocking collectives: 16.2 us -> none
    select_n x16 -> x0, other arithmetic: 15.9 us -> none  [turn(): return jax.tree.map(lambda a, b: jnp.where(reached, a, b), new, before)]
  transfers between devices with their start and end apart: 7 -> 0, of which waited for: 6 -> 0; matrix products, arithmetic and copies ran while one was open for 11% -> 0% of each run, Pallas kernels for 0% -> 0%
where the time goes in v2:
time: 158 us
  Pallas kernels  157 us (99%)
  local copies, waits for them, and re-layouts  1.62 us (1%)
    pallas_call x1, Pallas kernels, body(): pl.pallas_call(functools.partial(whole_kernel, names), out_shape=jax.Shap...  157 us

profile of v2, /device:TPU:1, one launch (start us, length us, event | category | flops | bytes accessed | tf_op | source)
XLA Modules:
  0.0 158.1 jit_solution(12904153305392591600)
XLA Ops:
  0.0 156.5 %mixer_grad.1 = bf16[24,4096]{1,0:T(8,128)(2,1)} custom-call(f32[2]{0:T(128)} %refs_0_.1, f32[2]{0:T(128)} %refs_1_.1, bf16[24,4096]{1,0:T(8,128)(2,1)} %refs_2_.1, bf16[24,4096]{1,0:T(8,128)(2,1)} %refs_3_.1, f32[4,256]{1,0:T(4,128)} %refs_4_.1, f32[4,256]{1,0:T(4,128)} %refs_5_.1, f32[1,256]{1,0:T(1,128)} %bitcast.3, bf16[2,4096,256]{2,1,0:T(8,128)(2,1)} %refs_7_.1, ...), custom_call_target="tpu_custom_call" | custom-call | tf_op jit(solution)/shard_map/mixer_grad/pallas_call | solution.py:946
  156.5 1.6 %copy.13 = bf16[24,4096]{1,0:T(8,128)(2,1)} copy(bf16[24,4096]{1,0:T(8,128)(2,1)} %mixer_grad.1) | data formatting | bytes 393216

commit v3 on v2

--- a/solution.py
+++ b/solution.py
@@ -13,6 +13,7 @@
 CONV = 4
 EPSILON = 1e-05
 EXACT = lax.Precision.HIGHEST
+NEAR = lax.Precision.HIGH
 MESH = pl.DeviceIdType.MESH
 F32 = jnp.float32
 BF16 = jnp.bfloat16
@@ -47,7 +48,7 @@
     )
 
 
-def dot(a, b, contract, precision=EXACT):
+def dot(a, b, contract, precision=NEAR):
     return lax.dot_general(a, b, (contract, ((), ())), precision=precision, preferred_element_type=F32)
 
 
@@ -206,17 +207,18 @@
             yt = self.yh if h == 0 else 1 - self.yh
             spots.append(pl.ds(pl.multiple_of((yt * Z + zt) * self.pair, 16), self.pair))
 
+        parts = []
+        for ref in (r.d_gate, r.d_inner, r.d_state, r.d_step):
+            parts.append(jnp.concatenate([ref[spots[0], :], ref[spots[1], :]], axis=0))
+
         def side(which, keep):
             def turn(j, carry):
                 here = pl.ds(pl.multiple_of(j * tile, tile), tile)
                 cols = pl.ds(pl.multiple_of(which * half + j * tile, tile), tile)
-                parts = []
-                for ref in (r.d_gate, r.d_inner, r.d_state, r.d_step):
-                    parts.append(jnp.concatenate([ref[spots[0], :], ref[spots[1], :]], axis=0))
-                value = dot16(parts[0], r.inner_w[0, cols, :], NT)
-                value += dot16(parts[1], r.inner_w[1, cols, :], NT)
-                value += dot16(parts[2], r.state_w[cols, :], NT)
-                value += dot16(parts[3], r.step_w[:, cols], NN)
+                value = dot16(parts[3], r.step_w[:, cols], NN)
+                for i in range(3):
+                    width = parts[i].shape[1]
+                    value += dot16(parts[i], r.rows_all[i * width : (i + 1) * width, cols], NN)
                 for h in (0, 1):
                     keep[at, h, :, here] = value[h * self.pair : (h + 1) * self.pair].astype(keep.dtype)
                 return carry
@@ -359,6 +361,67 @@
             copy.wait_send()
 
 
+class Turned:
+    def __init__(self, r):
+        self.r = r
+        self.size = r.stage.shape[1]
+        self.blocks = r.step_w.shape[1] // self.size
+        self.todo = [functools.partial(self.out_block, j) for j in range(self.blocks)]
+        self.copies = []
+        for i, ref in enumerate((r.inner_w.at[0], r.inner_w.at[1], r.state_w)):
+            self.todo += [functools.partial(self.block, i, ref, j) for j in range(self.blocks)]
+
+    def span(self, j):
+        return slice(j * self.size, (j + 1) * self.size)
+
+    def out_load(self, j):
+        r = self.r
+        return pltpu.make_async_copy(r.out_hbm.at[:, self.span(j)], r.stage.at[j % 2], r.stage_sem.at[j % 2])
+
+    def begin(self):
+        for j in (0, 1):
+            self.out_load(j).start()
+
+    def out_block(self, j):
+        self.out_load(j).wait()
+        self.r.out_t[self.span(j), :] = self.r.stage[j % 2].T
+        if j + 2 < self.blocks:
+            self.out_load(j + 2).start()
+
+    def block(self, i, ref, j):
+        slot = len(self.copies) % 4
+        if len(self.copies) >= 4:
+            self.copies[-4].wait()
+        self.r.stage[2 + slot] = ref[self.span(j), :].T
+        copy = pltpu.make_async_copy(
+            self.r.stage.at[2 + slot], self.r.turned_hbm.at[i, :, self.span(j)], self.r.stage_sem.at[2 + slot]
+        )
+        copy.start()
+        self.copies.append(copy)
+
+    def some(self, count):
+        for _ in range(count):
+            if self.todo:
+                self.todo.pop(0)()
+
+    def finish(self):
+        self.some(len(self.todo))
+        for copy in self.copies[-4:]:
+            copy.wait()
+
+    def back(self):
+        width = self.r.inner_w.shape[2]
+        loads = [
+            pltpu.make_async_copy(
+                self.r.turned_hbm.at[i], self.r.rows_all.at[i * width : (i + 1) * width, :], self.r.back_sem.at[i]
+            )
+            for i in range(3)
+        ]
+        for load in loads:
+            load.start()
+        return loads
+
+
 class Exchange:
     def __init__(self, out, into, cross_out, cross_in, send_sem, recv_sem, factors_in, heads, forward):
         self.ctx = lax.axis_index("ctx")
@@ -475,7 +538,7 @@
         step = jnp.maximum(raw, 0.0) + jnp.log1p(jnp.exp(-jnp.abs(raw)))
         step = jnp.where(valid, step, 0.0)
         r.steps[span(k), :] = step
-        cum = dot(causal, -step * rate, NN)
+        cum = dot(causal, -step * rate, NN, EXACT)
         r.cums[span(k), :] = cum
         turned = cum.T
         ends.append([cum[CHUNK - 1 :, h : h + 1] for h in range(heads)])
@@ -703,7 +766,7 @@
             pulls = jnp.where(f.lane == h, met - step * fed, pulls)
             feeds = jnp.where(f.lane == h, fed, feeds)
             edge = jnp.where(f.lane == h, jnp.sum(d_next * r.states[k + 1, h]), edge)
-        d_decay = dot(anti, pulls, NN) + edge
+        d_decay = dot(anti, pulls, NN, EXACT) + edge
         raw = jnp.where(f.valid, r.stepraw[span(k), :], 0.0) + f.bias
         d_raw = (feeds - f.rate * d_decay) * jax.nn.sigmoid(raw)
         r.d_step[span(k), :] = d_raw[:, :heads].astype(BF16)
@@ -748,11 +811,13 @@
     loads = [
         pltpu.make_async_copy(src, dst, r.weight_sem.at[i])
         for i, (src, dst) in enumerate(
-            ((r.inner_hbm, r.inner_w), (r.state_hbm, r.state_w), (r.out_hbm, r.out_w), (r.step_hbm, r.step_w))
+            ((r.inner_hbm, r.inner_w), (r.state_hbm, r.state_w), (r.step_hbm, r.step_w))
         )
     ]
     for load in loads:
         load.start()
+    turned = Turned(r)
+    turned.begin()
     yh, z, core = place()
     ctx = lax.axis_index("ctx")
     barrier = pltpu.get_barrier_semaphore()
@@ -772,15 +837,18 @@
     second.first_swap()
     first.begin()
     early, late = first.steps()[:-3], first.steps()[-3:]
+    turned.some(6)
+    for load in loads:
+        load.wait()
     for step in early:
         step()
+        turned.some(4)
     second.begin()
     pending = second.steps()
     for step in late:
         step()
         pending.pop(0)()
-    for load in loads:
-        load.wait()
+    turned.finish()
     first.finish()
 
     def tick():
@@ -811,20 +879,23 @@
     project(r.conv, width, r.state_w, r.rows_all, NN)
     project(r.stepraw, 0, r.step_w, r.rows_all, NT)
     project(r.gate, 0, r.inner_w.at[0], r.rows_all, NN)
+    first.drain()
+    weights = turned.back()
     f = mixer_forward(r, tick)
     while pending:
         tick()
     second.finish()
-    project(r.local, 0, r.out_w, r.grads_all, NT)
+    project(r.local, 0, r.out_t, r.grads_all, NN)
     sums, total_copies = token_sums(r, f)
     drain = mixer_backward(r, f, sums)
+    for load in weights:
+        load.wait()
     rows, depth = r.result.shape
     Scatter(r, rows, depth).run(r.result)
     f.drain()
     drain()
     for copy in total_copies:
         copy.wait_send()
-    first.drain()
     second.drain()
 
 
@@ -873,7 +944,8 @@
         "swaps": ((2, count, half), BF16),
         "inner_w": (inner_weight.shape, BF16),
         "state_w": (state_weight.shape, BF16),
-        "out_w": (out_weight.shape, BF16),
+        "out_t": (out_weight.shape[::-1], BF16),
+        "stage": ((6, width, width), BF16),
         "step_w": (step_weight.shape[::-1], BF16),
         "gate": ((total, width), BF16),
         "conv": ((total, both), BF16),
@@ -921,7 +993,9 @@
         "last_in": ((2, count, quarter), BF16),
     }
     semaphores = {
-        "weight_sem": 4,
+        "weight_sem": 3,
+        "stage_sem": 6,
+        "back_sem": 3,
         "send_r": 63,
         "recv_r": 63,
         "send_g": 63,
@@ -942,17 +1016,20 @@
         "last_send": 2,
         "last_recv": 2,
     }
-    names = list(inputs) + ["result"] + list(scratch) + list(semaphores)
+    names = list(inputs) + ["result", "turned_hbm"] + list(scratch) + list(semaphores)
     return pl.pallas_call(
         functools.partial(whole_kernel, names),
-        out_shape=jax.ShapeDtypeStruct((count, depth), BF16),
+        out_shape=(
+            jax.ShapeDtypeStruct((count, depth), BF16),
+            jax.ShapeDtypeStruct((3, width, depth), BF16),
+        ),
         in_specs=[spec for _, spec in inputs.values()],
-        out_specs=vmem,
+        out_specs=(vmem, anywhere),
         scratch_shapes=[pltpu.VMEM(shape, dtype) for shape, dtype in scratch.values()]
         + [pltpu.SemaphoreType.DMA((n,)) for n in semaphores.values()],
         compiler_params=pltpu.CompilerParams(collective_id=0, has_side_effects=True, vmem_limit_bytes=VMEM_LIMIT),
         name="mixer_grad",
-    )(*[value for value, _ in inputs.values()])
+    )(*[value for value, _ in inputs.values()])[0]
 
 
 def solution(mesh):

time: 158 us -> 152 us (0.962)
  Pallas kernels: 157 us -> 150 us
    pallas_call x1, Pallas kernels: 157 us -> 150 us  [body(): pl.pallas_call(functools.partial(whole_kernel, names), out_shape=(jax.Sha...]
where the time goes in v3:
time: 152 us; the launch traced here: 151 us
  Pallas kernels  150 us (99%)
  local copies, waits for them, and re-layouts  1.62 us (1%)
    pallas_call x1, Pallas kernels, body(): pl.pallas_call(functools.partial(whole_kernel, names), out_shape=(jax.Sha...  150 us

profile of v3, /device:TPU:1, one launch (start us, length us, event | category | flops | bytes accessed | tf_op | source)
XLA Modules:
  0.0 151.3 jit_solution(9333095721696315629)
XLA Ops:
  0.0 149.7 %mixer_grad.1 = (bf16[24,4096]{1,0:T(8,128)(2,1)}, bf16[3,256,4096]{2,1,0:T(8,128)(2,1)}) custom-call(f32[2]{0:T(128)} %refs_0_.1, f32[2]{0:T(128)} %refs_1_.1, bf16[24,4096]{1,0:T(8,128)(2,1)} %refs_2_.1, bf16[24,4096]{1,0:T(8,128)(2,1)} %refs_3_.1, f32[4,256]{1,0:T(4,128)} %refs_4_.1, f32[4,256]{1,0:T(4,128)} %refs_5_.1, f32[1,256]{1,0:T(1,128)} %bitcast.3, ...), custom_call_target="tpu_custom_call" | custom-call | tf_op jit(solution)/shard_map/mixer_grad/pallas_call | solution.py:1020
  149.7 1.6 %copy.13 = bf16[24,4096]{1,0:T(8,128)(2,1)} copy(bf16[24,4096]{1,0:T(8,128)(2,1)} %get-tuple-element.6) | data formatting | bytes 393216

commit v4 on v3

--- a/solution.py
+++ b/solution.py
@@ -293,41 +293,40 @@
             for sub in (0, 1):
                 self.message(kind, sub, d)
 
+        self.product(-4)
         self.product(-3)
-        self.product(3)
+        self.sib_got(-4)
+        both("y", 4)
         self.sib_got(-3)
         self.message("long", 0, 5)
         self.message("other", 0, 3)
-        self.message("y", 1, 3)
-        self.product(-4)
+        self.product(3)
         self.sib_got(3)
         self.message("long", 1, 5)
         self.message("other", 1, 3)
-        self.message("y", 0, 3)
+        both("y", 3)
         self.product(2)
-        self.sib_got(-4)
-        both("y", 4)
+        both("long", 4)
         self.product(-2)
-        both("long", 4)
         self.sib_got(2)
         self.message("short", 1, 2)
         self.message("y", 0, 2)
         self.sib_got(-2)
         self.message("short", 0, 2)
         self.message("y", 1, 2)
+        both("other", 2)
         self.product(1)
-        both("other", 2)
         both("long", 3)
         self.product(-1)
         self.sib_got(1)
         self.sib_got(-1)
         both("y", 1)
         both("other", 1)
-        both("short", 1)
         self.product(0)
         both("long", 2)
         self.sib_got(0)
         both("y", 0)
+        both("short", 1)
         both("long", 1)
         first = core == 0
         for sub in (0, 1):
@@ -501,7 +500,7 @@
             self.cross.wait_send()
 
 
-def mixer_forward(r, tick):
+def mixer_forward(r, tick, while_sent, while_crossing):
     ctx = lax.axis_index("ctx")
     total, both = r.conv.shape
     width = both - 2 * STATE
@@ -615,12 +614,12 @@
         if k % 3 == 2:
             tick()
 
+    while_sent()
     for copy in factor_copies:
         copy.wait_recv()
     forward.give(r.entering, r.states.at[chunks], factors)
-    tick()
+    while_crossing()
     forward.take(r.entering)
-    tick()
     for k in range(chunks):
         c_rows = r.act[span(k), width + STATE :]
         for h in range(heads):
@@ -628,8 +627,6 @@
             grown = jnp.exp(r.cums[span(k), h : h + 1] + befores[k][h])
             r.out[span(k), lanes] = r.out[span(k), lanes] + grown * dot(c_rows, r.entering[h], NT)
             r.states[k, h] = r.states[k, h] + jnp.exp(befores[k][h]) * r.entering[h]
-        if k % 2 == 1:
-            tick()
     for h in range(heads):
         r.states[chunks, h] = r.states[chunks, h] + whole[h] * r.entering[h]
 
@@ -878,14 +875,20 @@
     project(r.conv, 0, r.inner_w.at[1], r.rows_all, NN)
     project(r.conv, width, r.state_w, r.rows_all, NN)
     project(r.stepraw, 0, r.step_w, r.rows_all, NT)
-    project(r.gate, 0, r.inner_w.at[0], r.rows_all, NN)
-    first.drain()
-    weights = turned.back()
-    f = mixer_forward(r, tick)
-    while pending:
-        tick()
-    second.finish()
-    project(r.local, 0, r.out_t, r.grads_all, NN)
+
+    def while_sent():
+        project(r.gate, 0, r.inner_w.at[0], r.rows_all, NN)
+        first.drain()
+        weights.extend(turned.back())
+
+    def while_crossing():
+        while pending:
+            tick()
+        second.finish()
+        project(r.local, 0, r.out_t, r.grads_all, NN)
+
+    weights = []
+    f = mixer_forward(r, tick, while_sent, while_crossing)
     sums, total_copies = token_sums(r, f)
     drain = mixer_backward(r, f, sums)
     for load in weights:

time: 152 us -> 141 us (0.928)
  Pallas kernels: 150 us -> 139 us
    pallas_call x1, Pallas kernels: 150 us -> 139 us  [body(): pl.pallas_call(functools.partial(whole_kernel, names), out_shape=(jax.Sha...]
where the time goes in v4:
time: 141 us
  Pallas kernels  139 us (99%)
  local copies, waits for them, and re-layouts  1.62 us (1%)
    pallas_call x1, Pallas kernels, body(): pl.pallas_call(functools.partial(whole_kernel, names), out_shape=(jax.Sha...  139 us

profile of v4, /device:TPU:1, one launch (start us, length us, event | category | flops | bytes accessed | tf_op | source)
XLA Modules:
  0.0 140.5 jit_solution(8545641850450918801)
XLA Ops:
  0.0 138.9 %mixer_grad.1 = (bf16[24,4096]{1,0:T(8,128)(2,1)}, bf16[3,256,4096]{2,1,0:T(8,128)(2,1)}) custom-call(f32[2]{0:T(128)} %refs_0_.1, f32[2]{0:T(128)} %refs_1_.1, bf16[24,4096]{1,0:T(8,128)(2,1)} %refs_2_.1, bf16[24,4096]{1,0:T(8,128)(2,1)} %refs_3_.1, f32[4,256]{1,0:T(4,128)} %refs_4_.1, f32[4,256]{1,0:T(4,128)} %refs_5_.1, f32[1,256]{1,0:T(1,128)} %bitcast.3, ...), custom_call_target="tpu_custom_call" | custom-call | tf_op jit(solution)/shard_map/mixer_grad/pallas_call | solution.py:1023
  138.9 1.6 %copy.13 = bf16[24,4096]{1,0:T(8,128)(2,1)} copy(bf16[24,4096]{1,0:T(8,128)(2,1)} %get-tuple-element.6) | data formatting | bytes 393216

commit v5 on v4

--- a/solution.py
+++ b/solution.py
@@ -833,7 +833,7 @@
     first.first_swap()
     second.first_swap()
     first.begin()
-    early, late = first.steps()[:-3], first.steps()[-3:]
+    early, late = first.steps()[:-1], first.steps()[-1:]
     turned.some(6)
     for load in loads:
         load.wait()

time: 141 us -> 140 us (level)
  no operation moved by 1% of the time
where the time goes in v5:
time: 140 us
  Pallas kernels  138 us (99%)
  local copies, waits for them, and re-layouts  1.62 us (1%)
    pallas_call x1, Pallas kernels, body(): pl.pallas_call(functools.partial(whole_kernel, names), out_shape=(jax.Sha...  138 us

profile of v5, /device:TPU:1, one launch (start us, length us, event | category | flops | bytes accessed | tf_op | source)
XLA Modules:
  0.0 139.6 jit_solution(3902160070562977928)
XLA Ops:
  0.0 138.0 %mixer_grad.1 = (bf16[24,4096]{1,0:T(8,128)(2,1)}, bf16[3,256,4096]{2,1,0:T(8,128)(2,1)}) custom-call(f32[2]{0:T(128)} %refs_0_.1, f32[2]{0:T(128)} %refs_1_.1, bf16[24,4096]{1,0:T(8,128)(2,1)} %refs_2_.1, bf16[24,4096]{1,0:T(8,128)(2,1)} %refs_3_.1, f32[4,256]{1,0:T(4,128)} %refs_4_.1, f32[4,256]{1,0:T(4,128)} %refs_5_.1, f32[1,256]{1,0:T(1,128)} %bitcast.3, ...), custom_call_target="tpu_custom_call" | custom-call | tf_op jit(solution)/shard_map/mixer_grad/pallas_call | solution.py:1023
  138.0 1.6 %copy.13 = bf16[24,4096]{1,0:T(8,128)(2,1)} copy(bf16[24,4096]{1,0:T(8,128)(2,1)} %get-tuple-element.6) | data formatting | bytes 393216
